TPU v7x, 32 devices: a whole 2x2x4 slice. The times are simulated.
32 devices in a mesh: rep: 4 (over y, x), shard: 8 (over z, core).
Axes of the slice: x: 2, y: 2, z: 4, core: 2. Of those that a mesh axis runs over, the one named last changes fastest.
Arguments:
- tokens: bfloat16 [4096, 768], P(('rep', 'shard')), may hold values from -6 to 6
- segment_ids: int32 [32, 128], P(('rep', 'shard')), may hold values from 0 to 3, never falling along the last dimension, each value on 1 to 64 neighbouring positions
- first_gain: bfloat16 [768], P('shard'), may hold values from 0.5 to 1.5
- first_shift: bfloat16 [768], P('shard'), may hold values from -3 to 3
- qkv_weight: bfloat16 [768, 2304], P('shard'), may hold values from -3 to 3, as said below
- qv_bias: bfloat16 [2, 768], P(None, 'shard'), may hold values from -3 to 3
- proj_weight: bfloat16 [768, 768], P('shard'), may hold values from -0.625 to 0.625
- proj_bias: bfloat16 [768], P('shard'), may hold values from -3 to 3
- second_gain: bfloat16 [768], P('shard'), may hold values from 0.5 to 1.5
- second_shift: bfloat16 [768], P('shard'), may hold values from -3 to 3
- fc_weight: bfloat16 [768, 3072], P('shard'), may hold values from -0.21875 to 0.21875
- fc_bias: bfloat16 [3072], P('shard'), may hold values from -3 to 3
- out_weight: bfloat16 [3072, 768], P('shard'), may hold values from -0.109375 to 0.109375
- out_bias: bfloat16 [768], P('shard'), may hold values from -3 to 3
- cotangent: bfloat16 [4096, 768], P(('rep', 'shard')), may hold values from -6 to 6
Outputs:
- block_output: bfloat16 [4096, 768], P(('rep', 'shard'))
- grad_tokens: float32 [4096, 768], P(('rep', 'shard'))
- grad_first_gain: float32 [768], P('shard')
- grad_first_shift: float32 [768], P('shard')
- grad_qkv_weight: float32 [768, 2304], P('shard')
- grad_qv_bias: float32 [2, 768], P(None, 'shard')
- grad_proj_weight: float32 [768, 768], P('shard')
- grad_proj_bias: float32 [768], P('shard')
- grad_second_gain: float32 [768], P('shard')
- grad_second_shift: float32 [768], P('shard')
- grad_fc_weight: float32 [768, 3072], P('shard')
- grad_fc_bias: float32 [3072], P('shard')
- grad_out_weight: float32 [3072, 768], P('shard')
- grad_out_bias: float32 [768], P('shard')
Inputs may be any that keep to these rules, and one draw needn't show every extreme that they name: `segment_ids`: each row holds 4 runs of equal numbers in rising order, each run 1 to 64 long, one of them exactly 64. `qkv_weight`: columns 0 to 767 project to queries, the next 768 columns to keys, the last 768 columns to values.
All inputs are finite; a program needn't handle non-finite values.
Results may differ from a plain program's by a relative error of at most 0.011.
Values may be sent and summed in bfloat16 or wider, within the bound.
A program may use at most 128 MiB of HBM per device.

v0:
```python
import math

import jax
import jax.numpy as jnp
from jax import lax
from jax.sharding import PartitionSpec as P

D = 768
HEADS = 12
HD = 64


EPSILON = 1e-05


def layer_norm(field, norm_gain, norm_shift):
    center = field - jnp.mean(field, axis=-1, keepdims=True)
    spread = jnp.mean(center * center, axis=-1, keepdims=True)
    return center * lax.rsqrt(spread + EPSILON) * norm_gain + norm_shift


def gelu_tanh(field):
    return jax.nn.gelu(field, approximate=True)


def head_split(matrix):
    return matrix.reshape(matrix.shape[0], HEADS, HD)


def masked_scores(query, keys, segments):
    rows = query.shape[0]
    scores = jnp.einsum(
        "qhd,khd->hqk", head_split(query), head_split(keys), preferred_element_type=jnp.float32
    ) * (1.0 / math.sqrt(HD))
    position = lax.iota(jnp.int32, rows)
    allowed = (segments[:, None] == segments[None, :]) & (position[None, :] <= position[:, None])
    return jnp.where(allowed[None], scores, -1e30)


def attend_forward(query, keys, values, segments):
    rows = query.shape[0]
    scores = masked_scores(query, keys, segments)
    row_max = jnp.max(scores, axis=-1, keepdims=True)
    row_total = jnp.sum(jnp.exp(scores - row_max), axis=-1, keepdims=True)
    logsum = row_max + jnp.log(row_total)
    probs = jnp.exp(scores - logsum).astype(jnp.bfloat16)
    attended = jnp.einsum(
        "hqk,khd->qhd", probs, head_split(values), preferred_element_type=jnp.float32
    )
    return (attended.reshape(rows, D).astype(jnp.bfloat16), logsum)


def attend_backward(query, keys, values, segments, attended, logsum, grad_attended):
    rows = query.shape[0]
    scores = masked_scores(query, keys, segments)
    weights = jnp.exp(scores - logsum)
    grad_heads = head_split(grad_attended)
    grad_values = jnp.einsum(
        "hqk,qhd->khd", weights.astype(jnp.bfloat16), grad_heads, preferred_element_type=jnp.float32
    )
    grad_probs = jnp.einsum(
        "qhd,khd->hqk", grad_heads, head_split(values), preferred_element_type=jnp.float32
    )
    delta = jnp.einsum(
        "qhd,qhd->hq", grad_heads, head_split(attended), preferred_element_type=jnp.float32
    )
    grad_scores = (weights * (grad_probs - delta[..., None]) * (1.0 / math.sqrt(HD))).astype(
        jnp.bfloat16
    )
    grad_query = jnp.einsum(
        "hqk,khd->qhd", grad_scores, head_split(keys), preferred_element_type=jnp.float32
    )
    grad_keys = jnp.einsum(
        "hqk,qhd->khd", grad_scores, head_split(query), preferred_element_type=jnp.float32
    )
    return (grad_query.reshape(rows, D), grad_keys.reshape(rows, D), grad_values.reshape(rows, D))


def per_device(
    tokens,
    segment_ids,
    first_gain,
    first_shift,
    qkv_weight,
    qv_bias,
    proj_weight,
    proj_bias,
    second_gain,
    second_shift,
    fc_weight,
    fc_bias,
    out_weight,
    out_bias,
    cotangent,
):
    segments = segment_ids[0]
    own_rows = tokens.shape[0]
    factor = 1.0 / math.sqrt(own_rows * lax.axis_size("rep") * lax.axis_size("shard"))
    gain_one, shift_one, qkv_full, qv_full, proj_full, proj_bias_full = (
        lax.all_gather(first_gain, "shard", axis=0, tiled=True),
        lax.all_gather(first_shift, "shard", axis=0, tiled=True),
        lax.all_gather(qkv_weight, "shard", axis=0, tiled=True),
        lax.all_gather(qv_bias, "shard", axis=1, tiled=True),
        lax.all_gather(proj_weight, "shard", axis=0, tiled=True),
        lax.all_gather(proj_bias, "shard", axis=0, tiled=True),
    )
    inputs = tokens.astype(jnp.float32)
    normed_f, first_back = jax.vjp(
        layer_norm, inputs, gain_one.astype(jnp.float32), shift_one.astype(jnp.float32)
    )
    normed_first = normed_f.astype(jnp.bfloat16)
    projected = jnp.dot(normed_first, qkv_full, preferred_element_type=jnp.float32)
    query = (projected[:, :D] + qv_full[0].astype(jnp.float32)).astype(jnp.bfloat16)
    keys = projected[:, D : 2 * D].astype(jnp.bfloat16)
    values = (projected[:, 2 * D :] + qv_full[1].astype(jnp.float32)).astype(jnp.bfloat16)
    attended, logsum = attend_forward(query, keys, values, segments)
    residual = (
        inputs
        + jnp.dot(attended, proj_full, preferred_element_type=jnp.float32)
        + proj_bias_full.astype(jnp.float32)
    )
    cot_f = cotangent.astype(jnp.float32)
    term_out_bias = jnp.sum(cot_f, axis=0) * factor
    gain_two, shift_two, fc_full, fc_bias_full, out_full, out_bias_full = (
        lax.all_gather(second_gain, "shard", axis=0, tiled=True),
        lax.all_gather(second_shift, "shard", axis=0, tiled=True),
        lax.all_gather(fc_weight, "shard", axis=0, tiled=True),
        lax.all_gather(fc_bias, "shard", axis=0, tiled=True),
        lax.all_gather(out_weight, "shard", axis=0, tiled=True),
        lax.all_gather(out_bias, "shard", axis=0, tiled=True),
    )
    normed_s, second_back = jax.vjp(
        layer_norm, residual, gain_two.astype(jnp.float32), shift_two.astype(jnp.float32)
    )
    normed_second = normed_s.astype(jnp.bfloat16)
    pre_act = jnp.dot(
        normed_second, fc_full, preferred_element_type=jnp.float32
    ) + fc_bias_full.astype(jnp.float32)
    activated, gelu_back = jax.vjp(gelu_tanh, pre_act)
    hidden = activated.astype(jnp.bfloat16)
    result = (
        residual
        + jnp.dot(hidden, out_full, preferred_element_type=jnp.float32)
        + out_bias_full.astype(jnp.float32)
    ).astype(jnp.bfloat16)
    fc_back, out_back = (
        lax.all_gather(fc_weight, "shard", axis=0, tiled=True),
        lax.all_gather(out_weight, "shard", axis=0, tiled=True),
    )
    term_out_weight = jnp.dot(hidden.T, cotangent, preferred_element_type=jnp.float32) * factor
    grad_hidden = jnp.dot(cotangent, out_back.T, preferred_element_type=jnp.float32)
    (grad_pre,) = gelu_back(grad_hidden)
    grad_pre_low = grad_pre.astype(jnp.bfloat16)
    term_fc_bias = jnp.sum(grad_pre, axis=0) * factor
    term_fc_weight = (
        jnp.dot(normed_second.T, grad_pre_low, preferred_element_type=jnp.float32) * factor
    )
    grad_normed_second = jnp.dot(grad_pre_low, fc_back.T, preferred_element_type=jnp.float32)
    grad_from_norm, second_gain_sum, second_shift_sum = second_back(grad_normed_second)
    term_second_gain = second_gain_sum * factor
    term_second_shift = second_shift_sum * factor
    qkv_back, proj_back = (
        lax.all_gather(qkv_weight, "shard", axis=0, tiled=True),
        lax.all_gather(proj_weight, "shard", axis=0, tiled=True),
    )
    grad_residual = cot_f + grad_from_norm
    grad_residual_low = grad_residual.astype(jnp.bfloat16)
    term_proj_bias = jnp.sum(grad_residual, axis=0) * factor
    term_proj_weight = (
        jnp.dot(attended.T, grad_residual_low, preferred_element_type=jnp.float32) * factor
    )
    grad_attended = jnp.dot(
        grad_residual_low, proj_back.T, preferred_element_type=jnp.float32
    ).astype(jnp.bfloat16)
    grad_query, grad_keys, grad_values = attend_backward(
        query, keys, values, segments, attended, logsum, grad_attended
    )
    term_qv_bias = jnp.stack([jnp.sum(grad_query, axis=0), jnp.sum(grad_values, axis=0)]) * factor
    grad_projected = jnp.concatenate([grad_query, grad_keys, grad_values], axis=1).astype(
        jnp.bfloat16
    )
    term_qkv_weight = (
        jnp.dot(normed_first.T, grad_projected, preferred_element_type=jnp.float32) * factor
    )
    grad_normed_first = jnp.dot(grad_projected, qkv_back.T, preferred_element_type=jnp.float32)
    grad_input_norm, first_gain_sum, first_shift_sum = first_back(grad_normed_first)
    term_first_gain = first_gain_sum * factor
    term_first_shift = first_shift_sum * factor
    grad_inputs = grad_residual + grad_input_norm
    every_share = (
        lax.psum_scatter(term_first_gain, "shard", scatter_dimension=0, tiled=True),
        lax.psum_scatter(term_first_shift, "shard", scatter_dimension=0, tiled=True),
        lax.psum_scatter(term_qkv_weight, "shard", scatter_dimension=0, tiled=True),
        lax.psum_scatter(term_qv_bias, "shard", scatter_dimension=1, tiled=True),
        lax.psum_scatter(term_proj_weight, "shard", scatter_dimension=0, tiled=True),
        lax.psum_scatter(term_proj_bias, "shard", scatter_dimension=0, tiled=True),
        lax.psum_scatter(term_second_gain, "shard", scatter_dimension=0, tiled=True),
        lax.psum_scatter(term_second_shift, "shard", scatter_dimension=0, tiled=True),
        lax.psum_scatter(term_fc_weight, "shard", scatter_dimension=0, tiled=True),
        lax.psum_scatter(term_fc_bias, "shard", scatter_dimension=0, tiled=True),
        lax.psum_scatter(term_out_weight, "shard", scatter_dimension=0, tiled=True),
        lax.psum_scatter(term_out_bias, "shard", scatter_dimension=0, tiled=True),
    )
    summed = lax.psum(
        (
            every_share[0],
            every_share[1],
            every_share[3],
            every_share[5],
            every_share[6],
            every_share[7],
            every_share[9],
            every_share[11],
        ),
        "rep",
    )
    mat_pieces = (
        lax.psum_scatter(every_share[2], "rep", scatter_dimension=1, tiled=True),
        lax.psum_scatter(every_share[4], "rep", scatter_dimension=1, tiled=True),
        lax.psum_scatter(every_share[8], "rep", scatter_dimension=1, tiled=True),
        lax.psum_scatter(every_share[10], "rep", scatter_dimension=1, tiled=True),
    )
    qkv_grad, proj_grad, fc_grad, out_grad = (
        lax.all_gather(mat_pieces[0], "rep", axis=1, tiled=True),
        lax.all_gather(mat_pieces[1], "rep", axis=1, tiled=True),
        lax.all_gather(mat_pieces[2], "rep", axis=1, tiled=True),
        lax.all_gather(mat_pieces[3], "rep", axis=1, tiled=True),
    )
    return (
        result,
        grad_inputs,
        summed[0],
        summed[1],
        qkv_grad,
        summed[2],
        proj_grad,
        summed[3],
        summed[4],
        summed[5],
        fc_grad,
        summed[6],
        out_grad,
        summed[7],
    )


def solution(mesh):
    return jax.shard_map(
        per_device,
        mesh=mesh,
        in_specs=(
            P(("rep", "shard"), None),
            P(("rep", "shard"), None),
            P("shard"),
            P("shard"),
            P("shard", None),
            P(None, "shard"),
            P("shard", None),
            P("shard"),
            P("shard"),
            P("shard"),
            P("shard", None),
            P("shard"),
            P("shard", None),
            P("shard"),
            P(("rep", "shard"), None),
        ),
        out_specs=(
            P(("rep", "shard"), None),
            P(("rep", "shard"), None),
            P("shard"),
            P("shard"),
            P("shard", None),
            P(None, "shard"),
            P("shard", None),
            P("shard"),
            P("shard"),
            P("shard"),
            P("shard", None),
            P("shard"),
            P("shard", None),
            P("shard"),
        ),
        check_vma=False,
    )
```

profile of v0, /device:TPU:0, one launch (start us, length us, event | category | flops | bytes accessed | tf_op | source)
XLA Modules:
  0.0 732.9 jit_solution(12829275811453125032)
XLA Ops:
  12.8 31.4 %all-reduce.15 = (bf16[768]{0:T(1024)(128)(2,1)S(1)}, bf16[768]{0:T(1024)(128)(2,1)S(1)}, bf16[768]{0:T(1024)(128)(2,1)S(1)}, bf16[768]{0:T(1024)(128)(2,1)}, bf...) all-reduce(bf16[768]{0:T(1024)(128)(2,1)S(1)} %dynamic-update-slice, ...), channel_id=1, replica_groups=mesh['rep'=4,'shard'=8] {'shard'}, use_global_device_ids=true, to_apply=%add.1 | all-reduce | flops 4608 | bytes 18432
  44.3 8.6 %all-gather = bf16[8,96,2]{1,2,0:T(2,128)(2,1)S(1)} all-gather(bf16[1,96,2]{1,2,0:T(2,128)(2,1)S(1)} %bitcast.101), channel_id=1, replica_groups=mesh['rep'=4,'shard'=8] {'shard'}, dimensions={0}, use_global_device_ids=true | all-gather | bytes 3456 | tf_op jit(solution)/shard_map/all_gather | solution.py:103
  52.9 12.7 %all-gather.1 = bf16[8,1,384]{2,1,0:T(2,128)(2,1)S(1)} all-gather(bf16[1,1,384]{2,1,0:T(2,128)(2,1)S(1)} %reshape.213), channel_id=1, replica_groups=mesh['rep'=4,'shard'=8] {'shard'}, dimensions={0}, use_global_device_ids=true | all-gather | bytes 6912 | tf_op jit(solution)/shard_map/all_gather | solution.py:128
  66.8 2.7 fusion.44
  71.0 6.8 all-gather.12.cloned.1.call-done
  77.7 1.7 fusion.56
  79.7 51.2 %all-gather.16.cloned.1.call-done = bf16[3072,768]{1,0:T(8,128)(2,1)} async-done(((bf16[384,768]{1,0:T(8,128)(2,1)}), bf16[3072,768]{1,0:T(8,128)(2,1)}) %all-gather.16.cloned.1.call-update) | async-done | bytes 4718608 | tf_op jit(solution)/shard_map/all_gather | solution.py:129
  130.9 5.1 fusion.57
  136.0 46.9 %all-gather.14.cloned.1.call-done = bf16[768,3072]{1,0:T(8,128)(2,1)} async-done(((bf16[96,3072]{1,0:T(8,128)(2,1)}), bf16[768,3072]{1,0:T(8,128)(2,1)}) %all-gather.14.cloned.1.call-update) | async-done | bytes 4718608 | tf_op jit(solution)/shard_map/all_gather | solution.py:127
  183.0 5.4 fusion.49
  188.4 0.9 copy-done.5
  189.3 5.1 convolution_multiply_fusion.2
  194.5 5.7 convolution_multiply_fusion.1
  200.5 0.9 copy-done.6
  201.3 4.7 multiply_reduce_fusion
  206.0 0.9 fusion.51
  207.0 1.9 convolution_multiply_fusion.3
  209.0 1.2 copy-done.2
  210.2 1.2 convolution_convert_fusion.1
  211.4 1.1 copy.58
  212.7 1.1 fusion.9
  215.0 4.1 convolution_multiply_fusion
  219.2 73.6 %reduce-scatter.22.cloned.1.call-done = f32[96,3072]{1,0:T(8,128)} async-done(((f32[768,3072]{1,0:T(8,128)}), f32[96,3072]{1,0:T(8,128)}) %reduce-scatter.22.cloned.1.call-update) | async-done | bytes 1179664 | tf_op jit(solution)/shard_map/reduce_scatter | solution.py:199
  292.9 100.0 %reduce-scatter.26.cloned.1.call-done = f32[384,768]{1,0:T(8,128)} async-done(((f32[3072,768]{1,0:T(8,128)}), f32[384,768]{1,0:T(8,128)}) %reduce-scatter.26.cloned.1.call-update) | async-done | bytes 1179664 | tf_op jit(solution)/shard_map/reduce_scatter | solution.py:201
  392.9 2.7 copy.87
  395.8 0.9 copy.83
  396.8 33.0 %reduce-scatter.20.cloned.1.call-done = f32[96,768]{1,0:T(8,128)} async-done(((f32[768,768]{1,0:T(8,128)}), f32[96,768]{1,0:T(8,128)}) %reduce-scatter.20.cloned.1.call-update) | async-done | bytes 294928 | tf_op jit(solution)/shard_map/reduce_scatter | solution.py:195
  429.9 1.9 copy.85
  431.8 76.8 %reduce-scatter.18.cloned.1.call-done = f32[96,2304]{1,0:T(8,128)} async-done(((f32[768,2304]{1,0:T(8,128)}), f32[96,2304]{1,0:T(8,128)}) %reduce-scatter.18.cloned.1.call-update) | async-done | bytes 884752 | tf_op jit(solution)/shard_map/reduce_scatter | solution.py:193
  508.7 2.6 copy.81
  511.3 27.2 %reduce-scatter.24.cloned.1.call-done = f32[96,768]{1,0:T(8,128)} async-done(((f32[96,3072]{1,0:T(8,128)}), f32[96,768]{1,0:T(8,128)}) %reduce-scatter.24.cloned.1.call-update) | async-done | bytes 294928 | tf_op jit(solution)/shard_map/reduce_scatter | solution.py:220
  539.9 3.4 fusion.48
  543.7 26.8 %reduce-scatter.34.cloned.1.call-done = f32[192,384]{1,0:T(8,128)} async-done(((f32[768,384]{1,0:T(8,128)}), f32[192,384]{1,0:T(8,128)}) %reduce-scatter.34.cloned.1.call-update) | async-done | bytes 294928
  570.5 1.0 convert_reduce_fusion.1
  571.5 29.0 %all-reduce.13 = (f32[768]{0:T(1024)S(1)}, f32[768]{0:T(1024)S(1)}, f32[768]{0:T(1024)S(1)}, f32[768]{0:T(1024)S(1)}, f32[768]{0:T(1024)S(1)}, /*index=5*/f32[3072]{0:T(1024)S(1)}, f32[768]{0:T(1024)S(1)}) all-reduce(f32[768]{0:T(1024)S(1)} %get-tuple-element.87, ...), channel_id=2, replica_groups=mesh['rep'=4,'shard'=8] {'shard'}, use_global_device_ids=true, to_apply=%region_11.12.clone | all-reduce | flops 7680 | bytes 61440
  601.0 4.1 fusion.12
  606.0 9.7 %all-reduce.14 = (f32[96]{0:T(128)}, f32[96]{0:T(128)}, f32[2,96]{1,0:T(2,128)}, f32[96]{0:T(128)}, f32[96]{0:T(128)}, /*index=5*/f32[96]{0:T(128)}, f32[384]{0:T(512)}, f32[96]{0:T(128)}) all-reduce(f32[96]{0:T(128)S(1)} %dynamic-slice.7, f32[96]{0:T(128)S(1)} %dynamic-slice.9, ...), channel_id=1, replica_groups=mesh['rep'=4,'shard'=8] {'rep'}, use_global_device_ids=true, to_apply=%region_12.13 | all-reduce | flops 1152 | bytes 9216 | tf_op jit(solution)/shard_map/psum | solution.py:204
  615.7 13.8 %reduce-scatter.32.cloned.1.call-done = f32[192,96]{1,0:T(8,128)} async-done(((f32[768,96]{1,0:T(8,128)}), f32[192,96]{1,0:T(8,128)}) %reduce-scatter.32.cloned.1.call-update) | async-done | bytes 73744
  629.5 9.4 %all_gather.65 = f32[96,768]{0,1:T(8,128)S(1)} all-gather(f32[96,192]{0,1:T(8,128)} %bitcast.96), channel_id=1, replica_groups=mesh['rep'=4,'shard'=8] {'rep'}, dimensions={1}, use_global_device_ids=true | all-gather | bytes 368640 | tf_op jit(solution)/shard_map/all_gather | solution.py:225
  638.9 0.9 copy.66
  639.8 22.0 %reduce-scatter.28.cloned.1.call-done = f32[576,96]{1,0:T(8,128)} async-done(((f32[2304,96]{1,0:T(8,128)}), f32[576,96]{1,0:T(8,128)}) %reduce-scatter.28.cloned.1.call-update) | async-done | bytes 221200
  661.8 1.1 copy.82
  662.9 16.1 %all-gather.2 = f32[4,576,96]{1,2,0:T(8,128)S(1)} all-gather(f32[1,576,96]{1,2,0:T(8,128)S(1)} %bitcast.86), channel_id=1, replica_groups=mesh['rep'=4,'shard'=8] {'rep'}, dimensions={0}, use_global_device_ids=true | all-gather | bytes 1105920 | tf_op jit(solution)/shard_map/all_gather | solution.py:224
  679.6 1.5 reshape.216
  681.2 11.9 %all-gather.18.cloned.1.call-done = f32[96,3072]{1,0:T(8,128)} async-done(((f32[96,768]{1,0:T(8,128)}), f32[96,3072]{1,0:T(8,128)}) %all-gather.18.cloned.1.call-update) | async-done | bytes 1179664 | tf_op jit(solution)/shard_map/all_gather | solution.py:226
  693.1 29.6 %all-gather.20.cloned.1.call-done = f32[384,768]{0,1:T(8,128)} async-done(((f32[384,192]{0,1:T(8,128)}), f32[384,768]{0,1:T(8,128)}) %all-gather.20.cloned.1.call-update) | async-done | bytes 1179664 | tf_op jit(solution)/shard_map/all_gather | solution.py:227
  722.7 2.7 copy.67
  725.3 1.0 copy.97
  (179 shorter events, 12.1 us)
Async XLA Ops:
  7.2 3.0 copy-start.31
  7.2 4.2 copy-start.36
  7.2 4.5 copy-start.37
  7.2 4.7 copy-start.38
  7.2 4.9 copy-start.39
  7.2 5.1 copy-start.40
  7.2 5.4 copy-start.41
  7.3 37.0 %copy-start.35 = (bf16[2,96]{1,0:T(2,128)(2,1)S(1)}, bf16[2,96]{1,0:T(2,128)(2,1)}, u32[]{:S(2)}) copy-start(bf16[2,96]{1,0:T(2,128)(2,1)} %param.20) | copy-start | bytes 1156
  7.3 45.7 %copy-start.32 = (bf16[384]{0:T(512)(128)(2,1)S(1)}, bf16[384]{0:T(512)(128)(2,1)}, u32[]{:S(2)}) copy-start(bf16[384]{0:T(512)(128)(2,1)} %param.26) | copy-start | bytes 2308
  7.3 59.0 %copy-start = (bf16[128,768]{1,0:T(8,128)(2,1)S(1)}, bf16[128,768]{1,0:T(8,128)(2,1)}, u32[]{:S(2)}) copy-start(bf16[128,768]{1,0:T(8,128)(2,1)} %param.15) | copy-start | bytes 589828
  7.3 59.4 %copy-start.30 = (s32[1,128]{1,0:T(1,128)S(1)}, s32[1,128]{1,0:T(1,128)}, u32[]{:S(2)}) copy-start(s32[1,128]{1,0:T(1,128)} %param.16) | copy-start | bytes 1540
  7.3 59.5 %all-gather.10.cloned.1.call-start = ((), (), s32[]{:S(2)}) async-start(), calls=%async_computation.9 | async-start | bytes 3981312 | tf_op jit(solution)/shard_map/all_gather | solution.py:102
  8.0 69.7 %all-gather.12.cloned.1.call-start = ((), (), s32[]{:S(2)}) async-start(), calls=%async_computation.10 | async-start | bytes 1327104 | tf_op jit(solution)/shard_map/all_gather | solution.py:104
  8.8 122.1 %all-gather.16.cloned.1.call-start = ((), (), s32[]{:S(2)}) async-start(), calls=%async_computation.12 | async-start | bytes 5308416 | tf_op jit(solution)/shard_map/all_gather | solution.py:129
  9.5 173.4 %all-gather.14.cloned.1.call-start = ((), (), s32[]{:S(2)}) async-start(), calls=%async_computation.11 | async-start | bytes 5308416 | tf_op jit(solution)/shard_map/all_gather | solution.py:127
  10.1 282.8 %reduce-scatter.22.cloned.1.call-start = ((), (), s32[]{:S(2)}) async-start(), calls=%async_computation.15 | async-start | bytes 10616832 | tf_op jit(solution)/shard_map/reduce_scatter | solution.py:199
  66.4 3.1 copy-start.18
  66.6 2.9 copy-start.33
  66.6 2.9 copy-start.22
  70.6 8.8 %copy-start.16 = (f32[12,128]{1,0:T(8,128)}, f32[12,128]{1,0:T(8,128)S(1)}, u32[]{:S(2)}) copy-start(f32[12,128]{1,0:T(8,128)S(1)} %log_add_fusion) | copy-start | bytes 18436
  70.6 60.3 %copy-start.1 = (bf16[128,768]{1,0:T(8,128)(2,1)S(1)}, bf16[128,768]{1,0:T(8,128)(2,1)}, u32[]{:S(2)}) copy-start(bf16[128,768]{1,0:T(8,128)(2,1)} %param.29) | copy-start | bytes 589828
  70.9 65.1 %copy-start.7 = (bf16[12,64,128]{2,1,0:T(8,128)(2,1)}, bf16[12,64,128]{2,1,0:T(8,128)(2,1)S(1)}, u32[]{:S(2)}) copy-start(bf16[12,64,128]{2,1,0:T(8,128)(2,1)S(1)} %convolution_convert_fusion.2) | copy-start | bytes 589828
  79.5 121.0 %copy-start.21 = (f32[128]{0:T(128)}, f32[128]{0:T(128)S(1)}, u32[]{:S(2)}) copy-start(f32[128]{0:T(128)S(1)} %broadcast_multiply_fusion.7) | copy-start | bytes 1540
  79.7 120.8 %copy-start.26 = (f32[128]{0:T(128)}, f32[128]{0:T(128)S(1)}, u32[]{:S(2)}) copy-start(f32[128]{0:T(128)S(1)} %fusion.40) | copy-start | bytes 1540
  79.7 103.2 %copy-start.25 = (f32[8,1,384]{2,1,0:T(1,128)S(1)}, f32[8,1,384]{2,1,0:T(1,128)}, u32[]{:S(2)}) copy-start(f32[8,1,384]{2,1,0:T(1,128)} %convert_element_type.101) | copy-start | bytes 36868
  188.4 6.1 copy-start.3
  194.4 198.5 %reduce-scatter.26.cloned.1.call-start = ((), (), s32[]{:S(2)}) async-start(), calls=%async_computation.18 | async-start | bytes 10616832 | tf_op jit(solution)/shard_map/reduce_scatter | solution.py:201
  200.2 6.8 copy-start.8
  200.2 229.7 %reduce-scatter.20.cloned.1.call-start = ((), (), s32[]{:S(2)}) async-start(), calls=%async_computation.14 | async-start | bytes 2654208 | tf_op jit(solution)/shard_map/reduce_scatter | solution.py:195
  207.0 2.1 copy-start.27
  208.9 3.7 copy-start.10
  209.0 299.7 %reduce-scatter.18.cloned.1.call-start = ((), (), s32[]{:S(2)}) async-start(), calls=%async_computation.13 | async-start | bytes 7962624 | tf_op jit(solution)/shard_map/reduce_scatter | solution.py:193
  211.4 2.4 copy-start.14
  211.4 2.8 copy-start.12
  219.2 319.4 %reduce-scatter.24.cloned.1.call-start = ((), (), s32[]{:S(2)}) async-start(), calls=%async_computation.16 | async-start | bytes 1474560 | tf_op jit(solution)/shard_map/reduce_scatter | solution.py:220
  292.9 277.6 %reduce-scatter.34.cloned.1.call-start = ((), (), s32[]{:S(2)}) async-start(), calls=%async_computation.23 | async-start | bytes 1474560
  395.6 209.5 %reduce-scatter.30.cloned.1.call-start = ((), (), s32[]{:S(2)}) async-start(), calls=%async_computation.21 | async-start | bytes 442368
  396.8 232.7 %reduce-scatter.32.cloned.1.call-start = ((), (), s32[]{:S(2)}) async-start(), calls=%async_computation.22 | async-start | bytes 491520
  431.8 106.8 %copy-start.29 = (bf16[768]{0:T(1024)(128)(2,1)S(1)}, bf16[768]{0:T(1024)(128)(2,1)}, u32[]{:S(2)}) copy-start(bf16[768]{0:T(1024)(128)(2,1)} %get-tuple-element.57) | copy-start | bytes 4612
  431.8 230.0 %reduce-scatter.28.cloned.1.call-start = ((), (), s32[]{:S(2)}) async-start(), calls=%async_computation.20 | async-start | bytes 1474560
  511.2 181.9 %all-gather.18.cloned.1.call-start = ((), (), s32[]{:S(2)}) async-start(), calls=%async_computation.17 | async-start | bytes 1474560 | tf_op jit(solution)/shard_map/all_gather | solution.py:226
  538.6 184.1 %all-gather.20.cloned.1.call-start = ((), (), s32[]{:S(2)}) async-start(), calls=%async_computation.19 | async-start | bytes 1474560 | tf_op jit(solution)/shard_map/all_gather | solution.py:227
  539.9 3.4 copy-start.34
  539.9 30.5 %copy-start.28 = (f32[128]{0:T(128)S(1)}, f32[128]{0:T(128)}, u32[]{:S(2)}) copy-start(f32[128]{0:T(128)} %copy-done.27) | copy-start | bytes 1540
  543.3 28.2 %copy-start.20 = (f32[768]{0:T(1024)S(1)}, f32[768]{0:T(1024)}, u32[]{:S(2)}) copy-start(f32[768]{0:T(1024)} %get-tuple-element.32) | copy-start | bytes 9220
  543.3 28.2 %copy-start.24 = (f32[3072]{0:T(1024)S(1)}, f32[3072]{0:T(1024)}, u32[]{:S(2)}) copy-start(f32[3072]{0:T(1024)} %get-tuple-element.60) | copy-start | bytes 36868
  543.4 57.7 %copy-start.4 = (f32[128,3072]{1,0:T(8,128)S(1)}, f32[128,3072]{1,0:T(8,128)}, u32[]{:S(2)}) copy-start(f32[128,3072]{1,0:T(8,128)} %copy-done.3) | copy-start | bytes 4718596
  693.1 32.2 %copy-start.15 = (f32[96,3072]{1,0:T(8,128)S(1)}, f32[96,3072]{1,0:T(8,128)}, u32[]{:S(2)}) copy-start(f32[96,3072]{1,0:T(8,128)} %all-gather.18.cloned.1.call-done) | copy-start | bytes 3538948
  (9 other events, 10.5 us)
Sparse Core Ops, SparseCore 0:
  9.8 44.7 all-gather.9
  56.2 21.5 all-gather.11
  79.4 51.4 all-gather.15
  132.4 50.5 all-gather.13
  194.5 98.2 reduce-scatter.21
  295.0 97.8 reduce-scatter.25
  395.2 34.5 reduce-scatter.19
  432.2 76.4 reduce-scatter.17
  511.6 26.9 reduce-scatter.23
  541.9 28.5 reduce-scatter.33
  573.3 30.7 reduce-scatter.29
  607.0 22.4 reduce-scatter.31
  633.2 28.5 reduce-scatter.27
  663.7 29.3 all-gather.17
  694.9 27.7 all-gather.19
where the time goes:
time: 734 us; the launch traced here: 733 us
  waiting for transfers between devices  523 us (71%)
  blocking collectives  117 us (16%)
  matrix products  48.1 us (7%)
  local copies, waits for them, and re-layouts  24.2 us (3%)
  between operations  16.7 us (2%)
    reduce_scatter x1, waiting for transfers between devices, per_device(): lax.psum_scatter(term_out_weight, 'shard', scatter_dimension=0, tiled=True)  100 us
    reduce_scatter x1, waiting for transfers between devices, per_device(): lax.psum_scatter(term_qkv_weight, 'shard', scatter_dimension=0, tiled=True)  76.8 us
    reduce_scatter x1, waiting for transfers between devices, per_device(): lax.psum_scatter(term_fc_weight, 'shard', scatter_dimension=0, tiled=True)  73.6 us
    unnamed x19, waiting for transfers between devices  65.3 us
    unnamed x2, blocking collectives  60.4 us
    all_gather x1, waiting for transfers between devices, per_device(): lax.all_gather(out_weight, 'shard', axis=0, tiled=True)  51.2 us
    all_gather x1, waiting for transfers between devices, per_device(): lax.all_gather(fc_weight, 'shard', axis=0, tiled=True)  46.9 us
    reduce_scatter x1, waiting for transfers between devices, per_device(): lax.psum_scatter(term_proj_weight, 'shard', scatter_dimension=0, tiled=True)  33 us
  transfers between devices with their start and end apart: 15, of which 13 were waited for; matrix products, arithmetic and copies ran while one was open for 8% of the time, Pallas kernels for 0%

commit v1 on v0

v1 whole, which is shorter than its diff:
```python
import math

import jax
import jax.numpy as jnp
from jax import lax
from jax.sharding import PartitionSpec as P

D = 768
HEADS = 12
HD = 64


EPSILON = 1e-05


def layer_norm(field, norm_gain, norm_shift):
    center = field - jnp.mean(field, axis=-1, keepdims=True)
    spread = jnp.mean(center * center, axis=-1, keepdims=True)
    return center * lax.rsqrt(spread + EPSILON) * norm_gain + norm_shift


def gelu_tanh(field):
    return jax.nn.gelu(field, approximate=True)


def head_split(matrix):
    return matrix.reshape(matrix.shape[0], HEADS, HD)


def masked_scores(query, keys, segments):
    rows = query.shape[0]
    scores = jnp.einsum(
        "qhd,khd->hqk", head_split(query), head_split(keys), preferred_element_type=jnp.float32
    ) * (1.0 / math.sqrt(HD))
    position = lax.iota(jnp.int32, rows)
    allowed = (segments[:, None] == segments[None, :]) & (position[None, :] <= position[:, None])
    return jnp.where(allowed[None], scores, -1e30)


def attend_forward(query, keys, values, segments):
    rows = query.shape[0]
    scores = masked_scores(query, keys, segments)
    row_max = jnp.max(scores, axis=-1, keepdims=True)
    row_total = jnp.sum(jnp.exp(scores - row_max), axis=-1, keepdims=True)
    logsum = row_max + jnp.log(row_total)
    probs = jnp.exp(scores - logsum).astype(jnp.bfloat16)
    attended = jnp.einsum(
        "hqk,khd->qhd", probs, head_split(values), preferred_element_type=jnp.float32
    )
    return (attended.reshape(rows, D).astype(jnp.bfloat16), logsum)


def attend_backward(query, keys, values, segments, attended, logsum, grad_attended):
    rows = query.shape[0]
    scores = masked_scores(query, keys, segments)
    weights = jnp.exp(scores - logsum)
    grad_heads = head_split(grad_attended)
    grad_values = jnp.einsum(
        "hqk,qhd->khd", weights.astype(jnp.bfloat16), grad_heads, preferred_element_type=jnp.float32
    )
    grad_probs = jnp.einsum(
        "qhd,khd->hqk", grad_heads, head_split(values), preferred_element_type=jnp.float32
    )
    delta = jnp.einsum(
        "qhd,qhd->hq", grad_heads, head_split(attended), preferred_element_type=jnp.float32
    )
    grad_scores = (weights * (grad_probs - delta[..., None]) * (1.0 / math.sqrt(HD))).astype(
        jnp.bfloat16
    )
    grad_query = jnp.einsum(
        "hqk,khd->qhd", grad_scores, head_split(keys), preferred_element_type=jnp.float32
    )
    grad_keys = jnp.einsum(
        "hqk,qhd->khd", grad_scores, head_split(query), preferred_element_type=jnp.float32
    )
    return (grad_query.reshape(rows, D), grad_keys.reshape(rows, D), grad_values.reshape(rows, D))


def per_device(
    tokens,
    segment_ids,
    first_gain,
    first_shift,
    qkv_weight,
    qv_bias,
    proj_weight,
    proj_bias,
    second_gain,
    second_shift,
    fc_weight,
    fc_bias,
    out_weight,
    out_bias,
    cotangent,
):
    low = jnp.bfloat16
    segments = segment_ids[0]
    own_rows = tokens.shape[0]
    shards = lax.axis_size("shard")
    reps = lax.axis_size("rep")
    factor = 1.0 / math.sqrt(own_rows * reps * shards)
    small = jnp.stack(
        [first_gain, first_shift, qv_bias[0], qv_bias[1], proj_bias, second_gain, second_shift, out_bias]
    )
    small_full = lax.all_gather(small, "shard", axis=1, tiled=True).astype(jnp.float32)
    gain_one, shift_one, q_bias, v_bias, proj_bias_full, gain_two, shift_two, out_bias_full = (
        small_full[i] for i in range(8)
    )
    qkv_full = lax.all_gather(qkv_weight, "shard", axis=0, tiled=True)
    proj_full = lax.all_gather(proj_weight, "shard", axis=0, tiled=True)
    fc_cols = lax.all_to_all(fc_weight, "shard", split_axis=1, concat_axis=0, tiled=True)
    cot_all = lax.all_gather(cotangent, "shard", axis=0, tiled=True)

    inputs = tokens.astype(jnp.float32)
    normed_f, first_back = jax.vjp(layer_norm, inputs, gain_one, shift_one)
    normed_first = normed_f.astype(low)
    projected = jnp.dot(normed_first, qkv_full, preferred_element_type=jnp.float32)
    query = (projected[:, :D] + q_bias).astype(low)
    keys = projected[:, D : 2 * D].astype(low)
    values = (projected[:, 2 * D :] + v_bias).astype(low)
    attended, logsum = attend_forward(query, keys, values, segments)
    residual = (
        inputs + jnp.dot(attended, proj_full, preferred_element_type=jnp.float32) + proj_bias_full
    )
    cot_f = cotangent.astype(jnp.float32)
    term_out_bias = jnp.sum(cot_f, axis=0) * factor
    normed_s, second_back = jax.vjp(layer_norm, residual, gain_two, shift_two)
    normed_second = normed_s.astype(low)
    normed_all = lax.all_gather(normed_second, "shard", axis=0, tiled=True)
    pre_act = jnp.dot(normed_all, fc_cols, preferred_element_type=jnp.float32) + fc_bias.astype(
        jnp.float32
    )
    activated, gelu_back = jax.vjp(gelu_tanh, pre_act)
    hidden = activated.astype(low)
    grad_hidden = jnp.dot(cot_all, out_weight.T, preferred_element_type=jnp.float32)
    (grad_pre,) = gelu_back(grad_hidden)
    grad_pre_low = grad_pre.astype(low)
    term_fc_bias = jnp.sum(grad_pre, axis=0) * factor
    grad_normed_part = jnp.dot(grad_pre_low, fc_cols.T, preferred_element_type=jnp.float32).astype(low)
    grad_normed_second = lax.psum_scatter(
        grad_normed_part, "shard", scatter_dimension=0, tiled=True
    ).astype(jnp.float32)
    out_part = jnp.dot(hidden, out_weight, preferred_element_type=jnp.float32).astype(low)
    out_sum = lax.psum_scatter(out_part, "shard", scatter_dimension=0, tiled=True).astype(jnp.float32)
    result = (residual + out_sum + out_bias_full).astype(low)
    term_out_weight = (
        jnp.dot(hidden.T, cot_all, preferred_element_type=jnp.float32) * factor
    ).astype(low)
    term_fc_weight = (
        jnp.dot(normed_all.T, grad_pre_low, preferred_element_type=jnp.float32) * factor
    ).astype(low)
    out_piece = lax.psum_scatter(term_out_weight, "rep", scatter_dimension=0, tiled=True)
    out_grad = lax.all_gather(out_piece, "rep", axis=0, tiled=True).astype(jnp.float32)
    fc_own = D // (shards * reps)
    fc_rows = term_fc_weight.reshape(shards, reps, fc_own, -1).swapaxes(0, 1).reshape(D, -1)
    fc_piece = lax.psum_scatter(fc_rows, "rep", scatter_dimension=0, tiled=True)
    fc_piece = lax.all_to_all(fc_piece, "shard", split_axis=0, concat_axis=1, tiled=True)
    fc_grad = lax.all_gather(fc_piece, "rep", axis=0, tiled=True).astype(jnp.float32)

    grad_from_norm, second_gain_sum, second_shift_sum = second_back(grad_normed_second)
    grad_residual = cot_f + grad_from_norm
    grad_residual_low = grad_residual.astype(low)
    term_proj_bias = jnp.sum(grad_residual, axis=0) * factor
    term_proj_weight = (
        jnp.dot(attended.T, grad_residual_low, preferred_element_type=jnp.float32) * factor
    ).astype(low)
    grad_attended = jnp.dot(
        grad_residual_low, proj_full.T, preferred_element_type=jnp.float32
    ).astype(low)
    grad_query, grad_keys, grad_values = attend_backward(
        query, keys, values, segments, attended, logsum, grad_attended
    )
    grad_projected = jnp.concatenate([grad_query, grad_keys, grad_values], axis=1).astype(low)
    term_qkv_weight = (
        jnp.dot(normed_first.T, grad_projected, preferred_element_type=jnp.float32) * factor
    ).astype(low)
    grad_normed_first = jnp.dot(grad_projected, qkv_full.T, preferred_element_type=jnp.float32)
    grad_input_norm, first_gain_sum, first_shift_sum = first_back(grad_normed_first)
    grad_inputs = grad_residual + grad_input_norm

    proj_share = lax.psum_scatter(term_proj_weight, "shard", scatter_dimension=0, tiled=True)
    qkv_share = lax.psum_scatter(term_qkv_weight, "shard", scatter_dimension=0, tiled=True)
    proj_piece = lax.psum_scatter(proj_share, "rep", scatter_dimension=0, tiled=True)
    qkv_piece = lax.psum_scatter(qkv_share, "rep", scatter_dimension=0, tiled=True)
    proj_grad = lax.all_gather(proj_piece, "rep", axis=0, tiled=True).astype(jnp.float32)
    qkv_grad = lax.all_gather(qkv_piece, "rep", axis=0, tiled=True).astype(jnp.float32)
    terms = jnp.stack(
        [
            first_gain_sum * factor,
            first_shift_sum * factor,
            jnp.sum(grad_query, axis=0) * factor,
            jnp.sum(grad_values, axis=0) * factor,
            term_proj_bias,
            second_gain_sum * factor,
            second_shift_sum * factor,
            term_out_bias,
        ]
    )
    sums, fc_bias_grad = lax.psum(
        (lax.psum_scatter(terms, "shard", scatter_dimension=1, tiled=True), term_fc_bias), "rep"
    )
    return (
        result,
        grad_inputs,
        sums[0],
        sums[1],
        qkv_grad,
        sums[2:4],
        proj_grad,
        sums[4],
        sums[5],
        sums[6],
        fc_grad,
        fc_bias_grad,
        out_grad,
        sums[7],
    )


def solution(mesh):
    return jax.shard_map(
        per_device,
        mesh=mesh,
        in_specs=(
            P(("rep", "shard"), None),
            P(("rep", "shard"), None),
            P("shard"),
            P("shard"),
            P("shard", None),
            P(None, "shard"),
            P("shard", None),
            P("shard"),
            P("shard"),
            P("shard"),
            P("shard", None),
            P("shard"),
            P("shard", None),
            P("shard"),
            P(("rep", "shard"), None),
        ),
        out_specs=(
            P(("rep", "shard"), None),
            P(("rep", "shard"), None),
            P("shard"),
            P("shard"),
            P("shard", None),
            P(None, "shard"),
            P("shard", None),
            P("shard"),
            P("shard"),
            P("shard"),
            P("shard", None),
            P("shard"),
            P("shard", None),
            P("shard"),
        ),
        check_vma=False,
    )
```

time: 734 us -> 456 us (0.62)
  waiting for transfers between devices: 523 us -> 305 us
  blocking collectives: 117 us -> 63.8 us
  local copies, waits for them, and re-layouts: 24.2 us -> 10.1 us
  other arithmetic: 3.75 us -> 15.5 us
  matrix products: 48.1 us -> 36.5 us
  starting transfers between devices: 0.78 us -> 8.85 us
    reduce_scatter x3 -> x4, waiting for transfers between devices: 201 us -> 114 us  [the longest x1 30.8 us: per_device(): lax.psum_scatter(out_part, 'shard', scatter_dimension=0, tiled=True)]
    unnamed x2 -> x0, blocking collectives: 60.4 us -> none
    all_gather x6 -> x4, waiting for transfers between devices: 146 us -> 98.3 us  [the longest x1 30.8 us: per_device(): cot_all = lax.all_gather(cotangent, 'shard', axis=0, tiled=True)]
    reduce_scatter x1, waiting for transfers between devices: 76.8 us -> 41.6 us  [per_device(): lax.psum_scatter(term_qkv_weight, 'shard', scatter_dimension=0, tiled=True)]
    unnamed x19 -> x16, waiting for transfers between devices: 65.3 us -> 41 us
    reduce_scatter x1, waiting for transfers between devices: 33 us -> 10.2 us  [per_device(): lax.psum_scatter(term_proj_weight, 'shard', scatter_dimension=0, tiled=True)]
    unnamed x116 -> x50, local copies, waits for them, and re-layouts: 21.8 us -> 4.42 us
    dot_general x8, matrix products: 34.8 us -> 25.3 us  [the longest x1 5.52 us: per_device(): jnp.dot(normed_all, fc_cols, preferred_element_type=jnp.float32)]
  transfers between devices with their start and end apart: 15 -> 15, of which waited for: 13 -> 13; matrix products, arithmetic and copies ran while one was open for 8% -> 10% of each run, Pallas kernels for 0% -> 0%
where the time goes in v1:
time: 456 us; the launch traced here: 455 us
  waiting for transfers between devices  305 us (67%)
  blocking collectives  63.8 us (14%)
  matrix products  36.5 us (8%)
  other arithmetic  15.5 us (3%)
  between operations  14.5 us (3%)
  local copies, waits for them, and re-layouts  10.1 us (2%)
  starting transfers between devices  8.85 us (2%)
    reduce_scatter x1, waiting for transfers between devices, per_device(): lax.psum_scatter(term_qkv_weight, 'shard', scatter_dimension=0, tiled=True)  41.6 us
    unnamed x16, waiting for transfers between devices  41 us
    all_gather x1, waiting for transfers between devices, per_device(): cot_all = lax.all_gather(cotangent, 'shard', axis=0, tiled=True)  30.8 us
    reduce_scatter x1, waiting for transfers between devices, per_device(): lax.psum_scatter(out_part, 'shard', scatter_dimension=0, tiled=True)  30.8 us
    reduce_scatter x1, waiting for transfers between devices, per_device(): lax.psum_scatter(grad_normed_part, 'shard', scatter_dimension=0, tiled=True)  30.1 us
    reduce_scatter x1, waiting for transfers between devices, per_device(): lax.psum_scatter(term_out_weight, 'rep', scatter_dimension=0, tiled=True)  26.9 us
    reduce_scatter x1, waiting for transfers between devices, per_device(): fc_piece = lax.psum_scatter(fc_rows, 'rep', scatter_dimension=0, tiled=True)  26.6 us
    all_gather x1, waiting for transfers between devices, per_device(): qkv_full = lax.all_gather(qkv_weight, 'shard', axis=0, tiled=True)  26.1 us
  transfers between devices with their start and end apart: 15, of which 13 were waited for; matrix products, arithmetic and copies ran while one was open for 10% of the time, Pallas kernels for 0%

profile of v1, /device:TPU:0, one launch (start us, length us, event | category | flops | bytes accessed | tf_op | source)
XLA Modules:
  0.0 454.6 jit_solution(13503436207554731537)
XLA Ops:
  9.5 1.0 convert_reduce_fusion.1
  10.5 1.1 fusion.26
  12.4 14.4 %all-gather = bf16[8,96,8]{1,2,0:T(8,128)(2,1)S(1)} all-gather(bf16[1,96,8]{1,2,0:T(8,128)(2,1)S(1)} %bitcast.120), channel_id=1, replica_groups=mesh['rep'=4,'shard'=8] {'shard'}, dimensions={0}, use_global_device_ids=true | all-gather | bytes 13824 | tf_op jit(solution)/shard_map/all_gather | solution.py:105
  27.9 26.1 %all-gather.6.cloned.1.call-done = bf16[768,2304]{1,0:T(8,128)(2,1)} async-done(((bf16[96,2304]{1,0:T(8,128)(2,1)}), bf16[768,2304]{1,0:T(8,128)(2,1)}) %all-gather.6.cloned.1.call-update) | async-done | bytes 3538960 | tf_op jit(solution)/shard_map/all_gather | solution.py:109
  54.0 2.8 fusion.45
  58.2 19.0 %all-gather.8.cloned.1.call-done = bf16[768,768]{1,0:T(8,128)(2,1)} async-done(((bf16[96,768]{1,0:T(8,128)(2,1)}), bf16[768,768]{1,0:T(8,128)(2,1)}) %all-gather.8.cloned.1.call-update) | async-done | bytes 1179664 | tf_op jit(solution)/shard_map/all_gather | solution.py:110
  77.2 1.8 fusion.56
  80.0 0.9 copy.98
  80.9 3.5 all-to-all-start
  84.5 30.8 %all-gather.12.cloned.1.call-done = bf16[1024,768]{1,0:T(8,128)(2,1)} async-done(((bf16[128,768]{1,0:T(8,128)(2,1)}), bf16[1024,768]{1,0:T(8,128)(2,1)}) %all-gather.12.cloned.1.call-update) | async-done | bytes 1572880 | tf_op jit(solution)/shard_map/all_gather | solution.py:112
  115.3 3.6 fusion.57
  118.9 22.4 %all-gather.10.cloned.1.call-done = bf16[1024,768]{1,0:T(8,128)(2,1)} async-done(((bf16[128,768]{1,0:T(8,128)(2,1)}), bf16[1024,768]{1,0:T(8,128)(2,1)}) %all-gather.10.cloned.1.call-update) | async-done | bytes 1572880 | tf_op jit(solution)/shard_map/all_gather | solution.py:129
  141.3 5.5 %fusion.50 = (f32[384]{0:T(512)}, bf16[1024,384]{1,0:T(8,128)(2,1)S(1)}, f32[1024,384]{1,0:T(8,128)}) fusion(f32[1024,384]{1,0:T(8,128)} %fusion.57, f32[384]{0:T(512)S(1)} %convert_element_type.105, bf16[1024,768]{1,0:T(8,128)(2,1)} %all-gather.10.cloned.1.call-done, bf16[768,384]{1,0:T(8,128)(2,1)S(1)} %bitcast.112), kind=kOutput, calls=%fused_computation.118 | convolution fusion | flops 612630144 | bytes 6097920 | tf_op jit(solution)/shard_map/dot_general | solution.py:130
  146.8 0.9 copy-done.22
  147.7 2.2 convolution_convert_fusion
  150.0 3.8 convolution_convert_fusion.1
  153.9 30.1 %reduce-scatter.18.cloned.1.call-done = bf16[128,768]{1,0:T(8,128)(2,1)} async-done(((bf16[1024,768]{1,0:T(8,128)(2,1)}), bf16[128,768]{1,0:T(8,128)(2,1)}) %reduce-scatter.18.cloned.1.call-update) | async-done | bytes 196624 | tf_op jit(solution)/shard_map/reduce_scatter | solution.py:140
  183.9 1.7 convert_reduce_fusion
  185.7 1.8 fusion.28
  187.5 30.8 %reduce-scatter.16.cloned.1.call-done = bf16[128,768]{1,0:T(8,128)(2,1)} async-done(((bf16[1024,768]{1,0:T(8,128)(2,1)}), bf16[128,768]{1,0:T(8,128)(2,1)}) %reduce-scatter.16.cloned.1.call-update) | async-done | bytes 196624 | tf_op jit(solution)/shard_map/reduce_scatter | solution.py:144
  218.2 2.5 fusion.52
  220.7 1.5 multiply_convert_fusion.1
  222.3 2.4 fusion.6
  224.7 0.9 copy.77
  226.2 1.2 convolution_convert_fusion.3
  227.4 1.1 copy.72
  230.2 3.0 multiply_convert_fusion
  233.4 1.3 copy-done.7
  234.7 3.2 fusion.7
  238.1 3.4 fusion.49
  242.1 0.9 copy.92
  243.1 10.2 %reduce-scatter.22.cloned.1.call-done = bf16[96,768]{1,0:T(8,128)(2,1)} async-done(((bf16[768,768]{1,0:T(8,128)(2,1)}), bf16[96,768]{1,0:T(8,128)(2,1)}) %reduce-scatter.22.cloned.1.call-update) | async-done | bytes 147472 | tf_op jit(solution)/shard_map/reduce_scatter | solution.py:181
  253.3 26.6 %reduce-scatter.24.cloned.1.call-done = bf16[192,384]{1,0:T(8,128)(2,1)} async-done(((bf16[768,384]{1,0:T(8,128)(2,1)}), bf16[192,384]{1,0:T(8,128)(2,1)}) %reduce-scatter.24.cloned.1.call-update) | async-done | bytes 147472 | tf_op jit(solution)/shard_map/reduce_scatter | solution.py:156
  279.9 4.6 %all-to-all-start.1 = ((bf16[8,24,384]{2,1,0:T(8,128)(2,1)}), bf16[8,24,384]{2,1,0:T(8,128)(2,1)S(1)}, u32[]{:S(2)}, u32[]{:S(2)}) async-start(bf16[8,24,384]{2,1,0:T(8,128)(2,1)} %bitcast.117), calls=%async_computation.6 | async-start | bytes 294912 | tf_op jit(solution)/shard_map/all_to_all | solution.py:157
  284.5 41.6 %reduce-scatter.20.cloned.1.call-done = bf16[96,2304]{1,0:T(8,128)(2,1)} async-done(((bf16[768,2304]{1,0:T(8,128)(2,1)}), bf16[96,2304]{1,0:T(8,128)(2,1)}) %reduce-scatter.20.cloned.1.call-update) | async-done | bytes 442384 | tf_op jit(solution)/shard_map/reduce_scatter | solution.py:182
  326.2 26.9 %reduce-scatter.26.cloned.1.call-done = bf16[96,768]{1,0:T(8,128)(2,1)} async-done(((bf16[384,768]{1,0:T(8,128)(2,1)}), bf16[96,768]{1,0:T(8,128)(2,1)}) %reduce-scatter.26.cloned.1.call-update) | async-done | bytes 147472 | tf_op jit(solution)/shard_map/reduce_scatter | solution.py:152
  353.0 10.2 %all_gather.35 = bf16[384,768]{1,0:T(8,128)(2,1)S(1)} all-gather(bf16[96,768]{1,0:T(8,128)(2,1)} %reduce-scatter.26.cloned.1.call-done), channel_id=1, replica_groups=mesh['rep'=4,'shard'=8] {'rep'}, dimensions={0}, use_global_device_ids=true | all-gather | bytes 737280 | tf_op jit(solution)/shard_map/all_gather | solution.py:153
  363.3 1.1 convert_element_type.124
  364.4 10.5 %all_gather.34 = bf16[96,3072]{1,0:T(8,128)(2,1)S(1)} all-gather(bf16[24,3072]{1,0:T(8,128)(2,1)S(1)} %bitcast.116), channel_id=1, replica_groups=mesh['rep'=4,'shard'=8] {'rep'}, dimensions={0}, use_global_device_ids=true | all-gather | bytes 737280 | tf_op jit(solution)/shard_map/all_gather | solution.py:158
  374.8 1.1 convert_element_type.122
  376.0 0.9 add_add_fusion.2
  376.9 9.2 %reduce-scatter.28.cloned.1.call-done = f32[96,8]{1,0:T(8,128)} async-done(((f32[768,8]{1,0:T(8,128)}), f32[96,8]{1,0:T(8,128)}) %reduce-scatter.28.cloned.1.call-update) | async-done | bytes 3088
  387.0 10.5 %all-reduce.2 = (f32[8,96]{1,0:T(8,128)S(1)}, f32[384]{0:T(512)}) all-reduce(f32[8,96]{1,0:T(8,128)S(1)} %copy.93, f32[384]{0:T(512)S(1)} %broadcast_multiply_fusion.8), channel_id=1, replica_groups=mesh['rep'=4,'shard'=8] {'rep'}, use_global_device_ids=true, to_apply=%region_21.22 | all-reduce | flops 1152 | bytes 9216 | tf_op jit(solution)/shard_map/psum | solution.py:199
  398.6 11.6 %reduce-scatter.32.cloned.1.call-done = bf16[24,768]{1,0:T(8,128)(2,1)} async-done(((bf16[96,768]{1,0:T(8,128)(2,1)}), bf16[24,768]{1,0:T(8,128)(2,1)}) %reduce-scatter.32.cloned.1.call-update) | async-done | bytes 36880
  410.2 8.5 %all_gather.33 = bf16[96,768]{1,0:T(8,128)(2,1)S(1)} all-gather(bf16[24,768]{1,0:T(8,128)(2,1)} %reduce-scatter.32.cloned.1.call-done), channel_id=1, replica_groups=mesh['rep'=4,'shard'=8] {'rep'}, dimensions={0}, use_global_device_ids=true | all-gather | bytes 184320 | tf_op jit(solution)/shard_map/all_gather | solution.py:185
  419.5 17.9 %reduce-scatter.30.cloned.1.call-done = bf16[24,2304]{1,0:T(8,128)(2,1)} async-done(((bf16[96,2304]{1,0:T(8,128)(2,1)}), bf16[24,2304]{1,0:T(8,128)(2,1)}) %reduce-scatter.30.cloned.1.call-update) | async-done | bytes 110608
  437.4 9.7 %all_gather.32 = bf16[96,2304]{1,0:T(8,128)(2,1)S(1)} all-gather(bf16[24,2304]{1,0:T(8,128)(2,1)} %reduce-scatter.30.cloned.1.call-done), channel_id=1, replica_groups=mesh['rep'=4,'shard'=8] {'rep'}, dimensions={0}, use_global_device_ids=true | all-gather | bytes 552960 | tf_op jit(solution)/shard_map/all_gather | solution.py:186
  447.1 1.0 convert_element_type.118
  (127 shorter events, 12.3 us)
Async XLA Ops:
  7.2 108.1 %copy-start = (bf16[384,768]{1,0:T(8,128)(2,1)S(1)}, bf16[384,768]{1,0:T(8,128)(2,1)}, u32[]{:S(2)}) copy-start(bf16[384,768]{1,0:T(8,128)(2,1)} %param.27) | copy-start | bytes 1769476
  7.2 46.8 %all-gather.6.cloned.1.call-start = ((), (), s32[]{:S(2)}) async-start(), calls=%async_computation.11 | async-start | bytes 3981312 | tf_op jit(solution)/shard_map/all_gather | solution.py:109
  7.9 69.2 %all-gather.8.cloned.1.call-start = ((), (), s32[]{:S(2)}) async-start(), calls=%async_computation.12 | async-start | bytes 1327104 | tf_op jit(solution)/shard_map/all_gather | solution.py:110
  8.7 106.6 %all-gather.12.cloned.1.call-start = ((), (), s32[]{:S(2)}) async-start(), calls=%async_computation.15 | async-start | bytes 1769472 | tf_op jit(solution)/shard_map/all_gather | solution.py:112
  9.4 131.9 %all-gather.10.cloned.1.call-start = ((), (), s32[]{:S(2)}) async-start(), calls=%async_computation.13 | async-start | bytes 1769472 | tf_op jit(solution)/shard_map/all_gather | solution.py:129
  10.5 46.3 %copy-start.10 = (f32[128]{0:T(128)}, f32[128]{0:T(128)S(1)}, u32[]{:S(2)}) copy-start(f32[128]{0:T(128)S(1)} %broadcast_multiply_fusion.10) | copy-start | bytes 1540
  11.6 45.1 %copy-start.20 = (f32[128]{0:T(128)}, f32[128]{0:T(128)S(1)}, u32[]{:S(2)}) copy-start(f32[128]{0:T(128)S(1)} %fusion.26) | copy-start | bytes 1540
  27.9 28.9 %copy-start.16 = (f32[128]{0:T(128)}, f32[128]{0:T(128)S(1)}, u32[]{:S(2)}) copy-start(f32[128]{0:T(128)S(1)} %fusion.40) | copy-start | bytes 1540
  57.1 1.1 copy-start.5
  57.2 0.9 copy-start.3
  57.4 19.7 %copy-start.1 = (bf16[128,768]{1,0:T(8,128)(2,1)S(1)}, bf16[128,768]{1,0:T(8,128)(2,1)}, u32[]{:S(2)}) copy-start(bf16[128,768]{1,0:T(8,128)(2,1)} %param.15) | copy-start | bytes 589828
  77.1 2.9 copy-start.9
  79.1 5.3 %copy-start.19 = (bf16[384]{0:T(512)(128)(2,1)S(1)}, bf16[384]{0:T(512)(128)(2,1)}, u32[]{:S(2)}) copy-start(bf16[384]{0:T(512)(128)(2,1)} %param.26) | copy-start | bytes 2308
  80.9 38.0 %all-to-all-start = ((bf16[96,8,384]{2,0,1:T(8,128)(2,1)}), bf16[96,8,384]{2,0,1:T(8,128)(2,1)S(1)}, u32[]{:S(2)}, u32[]{:S(2)}) async-start(bf16[96,8,384]{2,0,1:T(8,128)(2,1)} %bitcast.91), calls=%async_computation | async-start | bytes 1179648 | tf_op jit(solution)/shard_map/all_to_all | solution.py:111
  84.4 99.5 %reduce-scatter.18.cloned.1.call-start = ((), (), s32[]{:S(2)}) async-start(), calls=%async_computation.16 | async-start | bytes 1769472 | tf_op jit(solution)/shard_map/reduce_scatter | solution.py:140
  146.8 0.9 copy-start.22
  149.9 68.3 %reduce-scatter.16.cloned.1.call-start = ((), (), s32[]{:S(2)}) async-start(), calls=%async_computation.14 | async-start | bytes 1769472 | tf_op jit(solution)/shard_map/reduce_scatter | solution.py:144
  153.8 64.5 %copy-start.8 = (bf16[128,768]{1,0:T(8,128)(2,1)S(1)}, bf16[128,768]{1,0:T(8,128)(2,1)}, u32[]{:S(2)}) copy-start(bf16[128,768]{1,0:T(8,128)(2,1)} %param.29) | copy-start | bytes 589828
  153.8 99.4 %reduce-scatter.22.cloned.1.call-start = ((), (), s32[]{:S(2)}) async-start(), calls=%async_computation.18 | async-start | bytes 1327104 | tf_op jit(solution)/shard_map/reduce_scatter | solution.py:181
  220.7 1.5 copy-start.23
  222.2 57.7 %reduce-scatter.24.cloned.1.call-start = ((), (), s32[]{:S(2)}) async-start(), calls=%async_computation.19 | async-start | bytes 737280 | tf_op jit(solution)/shard_map/reduce_scatter | solution.py:156
  224.7 1.5 copy-start.2
  225.6 100.5 %reduce-scatter.20.cloned.1.call-start = ((), (), s32[]{:S(2)}) async-start(), calls=%async_computation.17 | async-start | bytes 3981312 | tf_op jit(solution)/shard_map/reduce_scatter | solution.py:182
  227.4 1.6 copy-start.6
  227.4 2.0 copy-start.4
  229.0 1.2 copy-start.11
  229.0 1.2 copy-start.17
  233.3 1.4 copy-start.7
  233.3 4.6 %copy-start.12 = (f32[768]{0:T(1024)S(1)}, f32[768]{0:T(1024)}, u32[]{:S(2)}) copy-start(f32[768]{0:T(1024)} %get-tuple-element.20) | copy-start | bytes 9220
  233.3 4.7 %copy-start.13 = (f32[768]{0:T(1024)S(1)}, f32[768]{0:T(1024)}, u32[]{:S(2)}) copy-start(f32[768]{0:T(1024)} %get-tuple-element.14) | copy-start | bytes 9220
  233.3 4.7 %copy-start.14 = (f32[768]{0:T(1024)S(1)}, f32[768]{0:T(1024)}, u32[]{:S(2)}) copy-start(f32[768]{0:T(1024)} %get-tuple-element.34) | copy-start | bytes 9220
  233.3 4.7 %copy-start.15 = (f32[768]{0:T(1024)S(1)}, f32[768]{0:T(1024)}, u32[]{:S(2)}) copy-start(f32[768]{0:T(1024)} %get-tuple-element.43) | copy-start | bytes 9220
  233.3 119.7 %reduce-scatter.26.cloned.1.call-start = ((), (), s32[]{:S(2)}) async-start(), calls=%async_computation.20 | async-start | bytes 737280 | tf_op jit(solution)/shard_map/reduce_scatter | solution.py:152
  237.9 148.2 %reduce-scatter.28.cloned.1.call-start = ((), (), s32[]{:S(2)}) async-start(), calls=%async_computation.21 | async-start | bytes 442368
  238.1 3.6 copy-start.21
  241.5 43.0 %copy-start.18 = (f32[384]{0:T(512)S(1)}, f32[384]{0:T(512)}, u32[]{:S(2)}) copy-start(f32[384]{0:T(512)} %get-tuple-element.32) | copy-start | bytes 4612
  243.0 167.2 %reduce-scatter.32.cloned.1.call-start = ((), (), s32[]{:S(2)}) async-start(), calls=%async_computation.23 | async-start | bytes 184320
  279.9 84.5 %all-to-all-start.1 = ((bf16[8,24,384]{2,1,0:T(8,128)(2,1)}), bf16[8,24,384]{2,1,0:T(8,128)(2,1)S(1)}, u32[]{:S(2)}, u32[]{:S(2)}) async-start(bf16[8,24,384]{2,1,0:T(8,128)(2,1)} %bitcast.117), calls=%async_computation.6 | async-start | bytes 294912 | tf_op jit(solution)/shard_map/all_to_all | solution.py:157
  284.5 152.9 %reduce-scatter.30.cloned.1.call-start = ((), (), s32[]{:S(2)}) async-start(), calls=%async_computation.22 | async-start | bytes 552960
Sparse Core Ops, SparseCore 0:
  9.7 44.2 all-gather.5
  55.6 21.4 all-gather.7
  78.8 36.4 all-gather.11
  117.4 23.8 all-gather.9
  150.0 33.8 reduce-scatter.17
  186.1 32.1 reduce-scatter.15
  222.3 30.8 reduce-scatter.21
  256.7 23.1 reduce-scatter.23
  282.3 43.7 reduce-scatter.19
  329.4 23.5 reduce-scatter.25
  355.4 30.6 reduce-scatter.27
  388.7 21.4 reduce-scatter.31
  413.1 24.2 reduce-scatter.29

commit v2 on v1

--- a/solution.py
+++ b/solution.py
@@ -8,6 +8,7 @@
 D = 768
 HEADS = 12
 HD = 64
+FF = 3072
 
 
 EPSILON = 1e-05
@@ -74,6 +75,28 @@
         "hqk,qhd->khd", grad_scores, head_split(query), preferred_element_type=jnp.float32
     )
     return (grad_query.reshape(rows, D), grad_keys.reshape(rows, D), grad_values.reshape(rows, D))
+
+
+def exchange(field, axis, split, concat):
+    return lax.all_to_all(field, axis, split_axis=split, concat_axis=concat, tiled=True)
+
+
+def sum_exchanged(field, axis):
+    parts = lax.axis_size(axis)
+    blocks = exchange(field.reshape((parts, -1) + field.shape[1:]), axis, 0, 0)
+    return jnp.sum(blocks.astype(jnp.float32), axis=0)
+
+
+def spread(field, axis):
+    parts = lax.axis_size(axis)
+    return exchange(jnp.broadcast_to(field[None], (parts,) + field.shape), axis, 0, 0)
+
+
+def by_replica(field, shards, reps):
+    rows = field.shape[0]
+    return (
+        field.reshape(shards, reps, rows // (shards * reps), -1).swapaxes(0, 1).reshape(rows, -1)
+    )
 
 
 def per_device(
@@ -106,27 +129,30 @@
     gain_one, shift_one, q_bias, v_bias, proj_bias_full, gain_two, shift_two, out_bias_full = (
         small_full[i] for i in range(8)
     )
-    qkv_full = lax.all_gather(qkv_weight, "shard", axis=0, tiled=True)
     proj_full = lax.all_gather(proj_weight, "shard", axis=0, tiled=True)
-    fc_cols = lax.all_to_all(fc_weight, "shard", split_axis=1, concat_axis=0, tiled=True)
-    cot_all = lax.all_gather(cotangent, "shard", axis=0, tiled=True)
+    qkv_cols = exchange(qkv_weight, "shard", 1, 0)
+    fc_cols = exchange(fc_weight, "shard", 1, 0)
+    qkv_bias = jnp.concatenate([q_bias, jnp.zeros_like(q_bias), v_bias])
+    width = qkv_cols.shape[1]
+    bias_cols = lax.dynamic_slice_in_dim(qkv_bias, lax.axis_index("shard") * width, width)
 
     inputs = tokens.astype(jnp.float32)
     normed_f, first_back = jax.vjp(layer_norm, inputs, gain_one, shift_one)
-    normed_first = normed_f.astype(low)
-    projected = jnp.dot(normed_first, qkv_full, preferred_element_type=jnp.float32)
-    query = (projected[:, :D] + q_bias).astype(low)
-    keys = projected[:, D : 2 * D].astype(low)
-    values = (projected[:, 2 * D :] + v_bias).astype(low)
+    first_all = lax.all_gather(normed_f.astype(low), "shard", axis=0, tiled=True)
+    cot_later, first_all = lax.optimization_barrier((cotangent, first_all))
+    cot_all = lax.all_gather(cot_later, "shard", axis=0, tiled=True)
+    projected_cols = jnp.dot(first_all, qkv_cols, preferred_element_type=jnp.float32) + bias_cols
+    projected = exchange(projected_cols.astype(low), "shard", 0, 1)
+    query = projected[:, :D]
+    keys = projected[:, D : 2 * D]
+    values = projected[:, 2 * D :]
     attended, logsum = attend_forward(query, keys, values, segments)
     residual = (
         inputs + jnp.dot(attended, proj_full, preferred_element_type=jnp.float32) + proj_bias_full
     )
     cot_f = cotangent.astype(jnp.float32)
-    term_out_bias = jnp.sum(cot_f, axis=0) * factor
     normed_s, second_back = jax.vjp(layer_norm, residual, gain_two, shift_two)
-    normed_second = normed_s.astype(low)
-    normed_all = lax.all_gather(normed_second, "shard", axis=0, tiled=True)
+    normed_all = lax.all_gather(normed_s.astype(low), "shard", axis=0, tiled=True)
     pre_act = jnp.dot(normed_all, fc_cols, preferred_element_type=jnp.float32) + fc_bias.astype(
         jnp.float32
     )
@@ -135,70 +161,79 @@
     grad_hidden = jnp.dot(cot_all, out_weight.T, preferred_element_type=jnp.float32)
     (grad_pre,) = gelu_back(grad_hidden)
     grad_pre_low = grad_pre.astype(low)
-    term_fc_bias = jnp.sum(grad_pre, axis=0) * factor
     grad_normed_part = jnp.dot(grad_pre_low, fc_cols.T, preferred_element_type=jnp.float32).astype(low)
-    grad_normed_second = lax.psum_scatter(
-        grad_normed_part, "shard", scatter_dimension=0, tiled=True
-    ).astype(jnp.float32)
+    grad_normed_low = lax.psum_scatter(grad_normed_part, "shard", scatter_dimension=0, tiled=True)
+    term_out_weight = jnp.dot(hidden.T, cot_all, preferred_element_type=jnp.float32) * factor
+    term_fc_weight = jnp.dot(normed_all.T, grad_pre_low, preferred_element_type=jnp.float32) * factor
     out_part = jnp.dot(hidden, out_weight, preferred_element_type=jnp.float32).astype(low)
-    out_sum = lax.psum_scatter(out_part, "shard", scatter_dimension=0, tiled=True).astype(jnp.float32)
-    result = (residual + out_sum + out_bias_full).astype(low)
-    term_out_weight = (
-        jnp.dot(hidden.T, cot_all, preferred_element_type=jnp.float32) * factor
-    ).astype(low)
-    term_fc_weight = (
-        jnp.dot(normed_all.T, grad_pre_low, preferred_element_type=jnp.float32) * factor
-    ).astype(low)
-    out_piece = lax.psum_scatter(term_out_weight, "rep", scatter_dimension=0, tiled=True)
-    out_grad = lax.all_gather(out_piece, "rep", axis=0, tiled=True).astype(jnp.float32)
-    fc_own = D // (shards * reps)
-    fc_rows = term_fc_weight.reshape(shards, reps, fc_own, -1).swapaxes(0, 1).reshape(D, -1)
-    fc_piece = lax.psum_scatter(fc_rows, "rep", scatter_dimension=0, tiled=True)
-    fc_piece = lax.all_to_all(fc_piece, "shard", split_axis=0, concat_axis=1, tiled=True)
-    fc_grad = lax.all_gather(fc_piece, "rep", axis=0, tiled=True).astype(jnp.float32)
+    out_part, attended_later, grad_normed_low = lax.optimization_barrier(
+        (out_part, attended, grad_normed_low)
+    )
+    grad_normed_second = grad_normed_low.astype(jnp.float32)
 
     grad_from_norm, second_gain_sum, second_shift_sum = second_back(grad_normed_second)
     grad_residual = cot_f + grad_from_norm
     grad_residual_low = grad_residual.astype(low)
-    term_proj_bias = jnp.sum(grad_residual, axis=0) * factor
-    term_proj_weight = (
-        jnp.dot(attended.T, grad_residual_low, preferred_element_type=jnp.float32) * factor
-    ).astype(low)
+    grad_residual_all = lax.all_gather(grad_residual_low, "shard", axis=0, tiled=True)
+    attended_cols = exchange(attended_later, "shard", 1, 0)
     grad_attended = jnp.dot(
         grad_residual_low, proj_full.T, preferred_element_type=jnp.float32
     ).astype(low)
+    result = (residual + sum_exchanged(out_part, "shard") + out_bias_full).astype(low)
+    out_piece = sum_exchanged(term_out_weight.astype(low), "rep").astype(low)
+    fc_piece = sum_exchanged(by_replica(term_fc_weight.astype(low), shards, reps), "rep").astype(low)
+    fc_piece = exchange(fc_piece, "shard", 0, 1)
+    ff_all = spread(jnp.concatenate([out_piece, fc_piece.reshape(-1, D)]), "rep").astype(jnp.float32)
+    out_rows = out_piece.shape[0]
+    out_grad = ff_all[:, :out_rows].reshape(-1, D)
+    fc_grad = ff_all[:, out_rows:].reshape(-1, FF)
+
     grad_query, grad_keys, grad_values = attend_backward(
         query, keys, values, segments, attended, logsum, grad_attended
     )
     grad_projected = jnp.concatenate([grad_query, grad_keys, grad_values], axis=1).astype(low)
-    term_qkv_weight = (
-        jnp.dot(normed_first.T, grad_projected, preferred_element_type=jnp.float32) * factor
-    ).astype(low)
-    grad_normed_first = jnp.dot(grad_projected, qkv_full.T, preferred_element_type=jnp.float32)
+    grad_cols = exchange(grad_projected, "shard", 1, 0)
+    grad_first_part = jnp.dot(grad_cols, qkv_cols.T, preferred_element_type=jnp.float32).astype(low)
+    grad_normed_first = lax.psum_scatter(
+        grad_first_part, "shard", scatter_dimension=0, tiled=True
+    ).astype(jnp.float32)
+    term_qkv_weight = jnp.dot(first_all.T, grad_cols, preferred_element_type=jnp.float32) * factor
+    term_proj_weight = (
+        jnp.dot(attended_cols.T, grad_residual_all, preferred_element_type=jnp.float32) * factor
+    )
+    proj_piece = sum_exchanged(term_proj_weight.astype(low), "rep").astype(low)
+    qkv_piece = sum_exchanged(by_replica(term_qkv_weight.astype(low), shards, reps), "rep").astype(low)
+    qkv_piece = exchange(qkv_piece, "shard", 0, 1)
+    attn_all = spread(jnp.concatenate([proj_piece, qkv_piece.reshape(-1, D)]), "rep").astype(
+        jnp.float32
+    )
+    proj_rows = proj_piece.shape[0]
+    proj_grad = attn_all[:, :proj_rows].reshape(-1, D)
+    qkv_grad = attn_all[:, proj_rows:].reshape(-1, 3 * D)
+
     grad_input_norm, first_gain_sum, first_shift_sum = first_back(grad_normed_first)
     grad_inputs = grad_residual + grad_input_norm
-
-    proj_share = lax.psum_scatter(term_proj_weight, "shard", scatter_dimension=0, tiled=True)
-    qkv_share = lax.psum_scatter(term_qkv_weight, "shard", scatter_dimension=0, tiled=True)
-    proj_piece = lax.psum_scatter(proj_share, "rep", scatter_dimension=0, tiled=True)
-    qkv_piece = lax.psum_scatter(qkv_share, "rep", scatter_dimension=0, tiled=True)
-    proj_grad = lax.all_gather(proj_piece, "rep", axis=0, tiled=True).astype(jnp.float32)
-    qkv_grad = lax.all_gather(qkv_piece, "rep", axis=0, tiled=True).astype(jnp.float32)
     terms = jnp.stack(
         [
-            first_gain_sum * factor,
-            first_shift_sum * factor,
-            jnp.sum(grad_query, axis=0) * factor,
-            jnp.sum(grad_values, axis=0) * factor,
-            term_proj_bias,
-            second_gain_sum * factor,
-            second_shift_sum * factor,
-            term_out_bias,
+            first_gain_sum,
+            first_shift_sum,
+            jnp.sum(grad_query, axis=0),
+            jnp.sum(grad_values, axis=0),
+            jnp.sum(grad_residual, axis=0),
+            second_gain_sum,
+            second_shift_sum,
+            jnp.sum(cot_f, axis=0),
         ]
     )
-    sums, fc_bias_grad = lax.psum(
-        (lax.psum_scatter(terms, "shard", scatter_dimension=1, tiled=True), term_fc_bias), "rep"
-    )
+    count = terms.shape[0]
+    terms = terms.reshape(count, shards, -1).swapaxes(0, 1).reshape(shards, -1)
+    own_terms = jnp.concatenate(
+        [jnp.sum(exchange(terms, "shard", 0, 0), axis=0), jnp.sum(grad_pre, axis=0)]
+    )
+    sums = jnp.sum(spread(own_terms, "rep"), axis=0) * factor
+    own_cols = D // shards
+    fc_bias_grad = sums[count * own_cols :]
+    sums = sums[: count * own_cols].reshape(count, own_cols)
     return (
         result,
         grad_inputs,

time: 456 us -> 428 us (0.939)
  waiting for transfers between devices: 305 us -> 229 us
  starting transfers between devices: 8.85 us -> 50.1 us
  local copies, waits for them, and re-layouts: 10.1 us -> 21.6 us
  blocking collectives: 63.8 us -> 54.8 us
    all_to_all x2 -> x14, waiting for transfers between devices: 0.01 us -> 145 us  [exchange(): lax.all_to_all(field, axis, split_axis=split, concat_axis=concat, tiled=T...]
    reduce_scatter x5 -> x1, waiting for transfers between devices: 136 us -> 0.02 us  [per_device(): lax.psum_scatter(grad_first_part, 'shard', scatter_dimension=0, tiled=True)]
    all_to_all x2 -> x14, starting transfers between devices: 8.14 us -> 49.8 us  [exchange(): lax.all_to_all(field, axis, split_axis=split, concat_axis=concat, tiled=T...]
    all_to_all x0 -> x2, blocking collectives: none -> 40.4 us  [exchange(): lax.all_to_all(field, axis, split_axis=split, concat_axis=concat, tiled=T...]
    unnamed x16 -> x7, waiting for transfers between devices: 41 us -> 1.46 us
    all_gather x4 -> x0, blocking collectives: 38.9 us -> none  [the longest x1 10.5 us: per_device(): lax.all_gather(fc_piece, 'rep', axis=0, tiled=True).astype(jnp.float32)]
    all_gather x3 -> x4, waiting for transfers between devices: 79.3 us -> 51.3 us  [the longest x1 26 us: per_device(): cot_all = lax.all_gather(cot_later, 'shard', axis=0, tiled=True)]
    all_gather x1, waiting for transfers between devices: 19 us -> 0.01 us  [per_device(): proj_full = lax.all_gather(proj_weight, 'shard', axis=0, tiled=True)]
  transfers between devices with their start and end apart: 15 -> 21, of which waited for: 13 -> 17; matrix products, arithmetic and copies ran while one was open for 10% -> 12% of each run, Pallas kernels for 0% -> 0%
where the time goes in v2:
time: 428 us; the launch traced here: 426 us
  waiting for transfers between devices  229 us (54%)
  blocking collectives  54.8 us (13%)
  starting transfers between devices  50.1 us (12%)
  matrix products  36.6 us (9%)
  local copies, waits for them, and re-layouts  21.6 us (5%)
  other arithmetic  18.6 us (4%)
  between operations  14.8 us (3%)
    all_to_all x14, waiting for transfers between devices, exchange(): lax.all_to_all(field, axis, split_axis=split, concat_axis=concat, tiled=T...  145 us
    all_to_all x14, starting transfers between devices, exchange(): lax.all_to_all(field, axis, split_axis=split, concat_axis=concat, tiled=T...  49.8 us
    all_to_all x2, blocking collectives, exchange(): lax.all_to_all(field, axis, split_axis=split, concat_axis=concat, tiled=T...  40.4 us
    reduce_scatter x1, waiting for transfers between devices, per_device(): lax.psum_scatter(grad_normed_part, 'shard', scatter_dimension=0, tiled=True)  31.6 us
    all_gather x1, waiting for transfers between devices, per_device(): cot_all = lax.all_gather(cot_later, 'shard', axis=0, tiled=True)  26 us
    all_gather x1, waiting for transfers between devices, per_device(): lax.all_gather(normed_s.astype(low), 'shard', axis=0, tiled=True)  23.8 us
    all_gather x1, blocking collectives, per_device(): lax.all_gather(small, 'shard', axis=1, tiled=True).astype(jnp.float32)  14.4 us
  transfers between devices with their start and end apart: 21, of which 17 were waited for; matrix products, arithmetic and copies ran while one was open for 12% of the time, Pallas kernels for 0%

profile of v2, /device:TPU:0, one launch (start us, length us, event | category | flops | bytes accessed | tf_op | source)
XLA Modules:
  0.0 425.8 jit_solution(18184944629674271424)
XLA Ops:
  10.8 14.4 %all-gather = bf16[8,96,8]{1,2,0:T(8,128)(2,1)S(1)} all-gather(bf16[1,96,8]{1,2,0:T(8,128)(2,1)S(1)} %bitcast.151), channel_id=1, replica_groups=mesh['rep'=4,'shard'=8] {'shard'}, dimensions={0}, use_global_device_ids=true | all-gather | bytes 13824 | tf_op jit(solution)/shard_map/all_gather | solution.py:128
  25.9 1.8 fusion.31
  29.5 3.5 all-to-all-start
  33.2 28.6 %all-to-all-done = bf16[96,8,288]{0,2,1:T(8,128)(2,1)S(1)} async-done(((bf16[96,8,288]{0,2,1:T(8,128)(2,1)}), bf16[96,8,288]{0,2,1:T(8,128)(2,1)S(1)}, u32[]{:S(2)}, u32[]{:S(2)}) %all-to-all-start) | async-done | bytes 442400 | tf_op jit(solution)/shard_map/all_to_all | solution.py:81
  62.5 1.4 all-gather.7.cloned.1.call-done
  64.0 2.1 fusion.13
  67.0 3.5 all-to-all-start.1
  71.4 25.3 %all-to-all-done.1 = bf16[8,128,288]{1,2,0:T(8,128)(2,1)S(1)} async-done(((bf16[8,128,288]{1,2,0:T(8,128)(2,1)}), bf16[8,128,288]{1,2,0:T(8,128)(2,1)S(1)}, u32[]{:S(2)}, u32[]{:S(2)}) %all-to-all-start.1) | async-done | bytes 589856 | tf_op jit(solution)/shard_map/all_to_all | solution.py:81
  98.8 1.9 fusion.61
  103.2 4.2 all-to-all-start.2
  108.0 26.0 %all-gather.13.cloned.1.call-done = bf16[1024,768]{1,0:T(8,128)(2,1)} async-done(((bf16[128,768]{1,0:T(8,128)(2,1)}), bf16[1024,768]{1,0:T(8,128)(2,1)}) %all-gather.13.cloned.1.call-update) | async-done | bytes 1572880 | tf_op jit(solution)/shard_map/all_gather | solution.py:143
  134.0 2.4 fusion.62
  136.4 23.8 %all-gather.11.cloned.1.call-done = bf16[1024,768]{1,0:T(8,128)(2,1)} async-done(((bf16[128,768]{1,0:T(8,128)(2,1)}), bf16[1024,768]{1,0:T(8,128)(2,1)}) %all-gather.11.cloned.1.call-update) | async-done | bytes 1572880 | tf_op jit(solution)/shard_map/all_gather | solution.py:155
  160.3 5.3 %fusion.52 = (f32[384]{0:T(512)}, bf16[1024,384]{1,0:T(8,128)(2,1)S(1)}, f32[1024,384]{1,0:T(8,128)}) fusion(f32[1024,384]{1,0:T(8,128)S(1)} %fusion.62, f32[384]{0:T(512)} %convert_element_type.112, bf16[1024,768]{1,0:T(8,128)(2,1)} %all-gather.11.cloned.1.call-done, bf16[768,384]{1,0:T(8,128)(2,1)} %bitcast.23), kind=kOutput, calls=%fused_computation.118 | convolution fusion | flops 612630144 | bytes 6097920 | tf_op jit(solution)/shard_map/dot_general | solution.py:156
  166.4 3.3 convolution_convert_fusion
  169.8 2.4 convolution_convert_fusion.1
  172.2 31.6 %reduce-scatter.3.cloned.1.call-done = bf16[128,768]{1,0:T(8,128)(2,1)} async-done(((bf16[1024,768]{1,0:T(8,128)(2,1)}), bf16[128,768]{1,0:T(8,128)(2,1)}) %reduce-scatter.3.cloned.1.call-update) | async-done | bytes 196624 | tf_op jit(solution)/shard_map/reduce_scatter | solution.py:165
  203.8 3.6 all-to-all-start.3
  207.4 1.8 fusion.35
  210.4 34.7 %all-to-all-done.3 = bf16[8,128,768]{2,1,0:T(8,128)(2,1)S(1)} async-done(((bf16[8,128,768]{2,1,0:T(8,128)(2,1)}), bf16[8,128,768]{2,1,0:T(8,128)(2,1)S(1)}, u32[]{:S(2)}, u32[]{:S(2)}) %all-to-all-start.3) | async-done | bytes 1572896 | tf_op jit(solution)/shard_map/all_to_all | solution.py:81
  247.8 1.5 convolution_convert_fusion.4
  254.2 28.8 %all_to_all.175 = bf16[128,8,288]{0,2,1:T(8,128)(2,1)S(1)} all-to-all(bf16[128,8,288]{0,2,1:T(8,128)(2,1)S(1)} %bitcast.131), channel_id=1, replica_groups=mesh['rep'=4,'shard'=8] {'shard'}, dimensions={1} | all-to-all | bytes 1179648 | tf_op jit(solution)/shard_map/all_to_all | solution.py:81
  283.0 2.2 convolution_convert_fusion.2
  286.3 2.4 fusion.7
  289.6 3.6 all-to-all-start.13
  293.3 3.7 fusion.6
  296.9 5.3 %all-to-all-done.13 = bf16[4,192,384]{2,1,0:T(8,128)(2,1)S(1)} async-done(((bf16[4,192,384]{2,1,0:T(8,128)(2,1)}), bf16[4,192,384]{2,1,0:T(8,128)(2,1)S(1)}, u32[]{:S(2)}, u32[]{:S(2)}) %all-to-all-start.13) | async-done | bytes 589856 | tf_op jit(solution)/shard_map/all_to_all | solution.py:81
  302.2 3.5 all-to-all-start.12
  306.5 7.5 %all-to-all-done.12 = bf16[4,96,768]{2,1,0:T(8,128)(2,1)S(1)} async-done(((bf16[4,96,768]{2,1,0:T(8,128)(2,1)}), bf16[4,96,768]{2,1,0:T(8,128)(2,1)S(1)}, u32[]{:S(2)}, u32[]{:S(2)}) %all-to-all-start.12) | async-done | bytes 589856 | tf_op jit(solution)/shard_map/all_to_all | solution.py:81
  314.0 3.4 all-to-all-start.14
  317.4 2.0 fusion.12
  319.8 4.5 %all-to-all-done.14 = bf16[8,24,384]{2,1,0:T(8,128)(2,1)S(1)} async-done(((bf16[8,24,384]{2,1,0:T(8,128)(2,1)}), bf16[8,24,384]{2,1,0:T(8,128)(2,1)S(1)}, u32[]{:S(2)}, u32[]{:S(2)}) %all-to-all-start.14) | async-done | bytes 147488 | tf_op jit(solution)/shard_map/all_to_all | solution.py:81
  324.3 11.6 %all_to_all.176 = bf16[4,192,288]{2,1,0:T(8,128)(2,1)S(1)} all-to-all(bf16[4,192,288]{2,1,0:T(8,128)(2,1)S(1)} %bitcast.130), channel_id=1, replica_groups=mesh['rep'=4,'shard'=8] {'rep'}, dimensions={0} | all-to-all | bytes 884736 | tf_op jit(solution)/shard_map/all_to_all | solution.py:81
  335.9 3.4 all-to-all-start.7
  340.3 7.3 %all-to-all-done.7 = bf16[128,8,96]{0,2,1:T(8,128)(2,1)S(1)} async-done(((bf16[128,8,96]{0,2,1:T(8,128)(2,1)}), bf16[128,8,96]{0,2,1:T(8,128)(2,1)S(1)}, u32[]{:S(2)}, u32[]{:S(2)}) %all-to-all-start.7) | async-done | bytes 196640 | tf_op jit(solution)/shard_map/all_to_all | solution.py:81
  347.6 3.4 all-to-all-start.10
  351.0 2.5 fusion.16
  353.5 4.4 %all-to-all-done.10 = bf16[8,24,288]{2,1,0:T(8,128)(2,1)S(1)} async-done(((bf16[8,24,288]{2,1,0:T(8,128)(2,1)}), bf16[8,24,288]{2,1,0:T(8,128)(2,1)S(1)}, u32[]{:S(2)}, u32[]{:S(2)}) %all-to-all-start.10) | async-done | bytes 110624 | tf_op jit(solution)/shard_map/all_to_all | solution.py:81
  357.9 3.3 all-to-all-start.8
  361.9 4.4 %all-to-all-done.8 = bf16[4,24,768]{2,1,0:T(8,128)(2,1)S(1)} async-done(((bf16[4,24,768]{2,1,0:T(8,128)(2,1)}), bf16[4,24,768]{2,1,0:T(8,128)(2,1)S(1)}, u32[]{:S(2)}, u32[]{:S(2)}) %all-to-all-start.8) | async-done | bytes 147488 | tf_op jit(solution)/shard_map/all_to_all | solution.py:81
  367.4 3.7 all-to-all-start.15
  373.7 1.9 convert_reduce_fusion.4
  376.6 8.2 %all-to-all-done.15 = bf16[4,192,768]{2,1,0:T(8,128)(2,1)S(1)} async-done(((bf16[4,192,768]{2,1,0:T(8,128)(2,1)}), bf16[4,192,768]{2,1,0:T(8,128)(2,1)S(1)}, u32[]{:S(2)}, u32[]{:S(2)}) %all-to-all-start.15) | async-done | bytes 1179680 | tf_op jit(solution)/shard_map/all_to_all | solution.py:81
  384.8 3.4 all-to-all-start.5
  388.1 5.7 %all-to-all-done.5 = f32[8,1,768]{2,1,0:T(1,128)S(1)} async-done(((f32[8,1,768]{2,1,0:T(1,128)}), f32[8,1,768]{2,1,0:T(1,128)S(1)}, u32[]{:S(2)}, u32[]{:S(2)}) %all-to-all-start.5) | async-done | bytes 24608 | tf_op jit(solution)/shard_map/all_to_all | solution.py:81
  394.7 3.5 all-to-all-start.11
  398.2 8.8 %all-to-all-done.11 = bf16[4,96,768]{2,1,0:T(8,128)(2,1)S(1)} async-done(((bf16[4,96,768]{2,1,0:T(8,128)(2,1)}), bf16[4,96,768]{2,1,0:T(8,128)(2,1)S(1)}, u32[]{:S(2)}, u32[]{:S(2)}) %all-to-all-start.11) | async-done | bytes 589856 | tf_op jit(solution)/shard_map/all_to_all | solution.py:81
  407.7 3.9 all-to-all-start.6
  (176 shorter events, 41.7 us)
Async XLA Ops:
  7.2 126.8 %copy-start = (bf16[384,768]{1,0:T(8,128)(2,1)S(1)}, bf16[384,768]{1,0:T(8,128)(2,1)}, u32[]{:S(2)}) copy-start(bf16[384,768]{1,0:T(8,128)(2,1)} %param.27) | copy-start | bytes 1769476
  7.2 21.3 %copy-start.12 = (bf16[96,2304]{1,0:T(8,128)(2,1)S(1)}, bf16[96,2304]{1,0:T(8,128)(2,1)}, u32[]{:S(2)}) copy-start(bf16[96,2304]{1,0:T(8,128)(2,1)} %param.19) | copy-start | bytes 1327108
  7.2 56.7 %all-gather.7.cloned.1.call-start = ((), (), s32[]{:S(2)}) async-start(), calls=%async_computation.18 | async-start | bytes 1769472 | tf_op jit(solution)/shard_map/all_gather | solution.py:141
  8.4 21.1 %copy-start.20 = (f32[128]{0:T(128)}, f32[128]{0:T(128)S(1)}, u32[]{:S(2)}) copy-start(f32[128]{0:T(128)S(1)} %broadcast_multiply_fusion.2) | copy-start | bytes 1540
  9.6 20.0 %copy-start.24 = (f32[128]{0:T(128)}, f32[128]{0:T(128)S(1)}, u32[]{:S(2)}) copy-start(f32[128]{0:T(128)S(1)} %fusion.48) | copy-start | bytes 1540
  27.7 71.1 %all-gather.9.cloned.1.call-start = ((), (), s32[]{:S(2)}) async-start(), calls=%async_computation.19 | async-start | bytes 1327104 | tf_op jit(solution)/shard_map/all_gather | solution.py:132
  29.5 32.3 %all-to-all-start = ((bf16[96,8,288]{0,2,1:T(8,128)(2,1)}), bf16[96,8,288]{0,2,1:T(8,128)(2,1)S(1)}, u32[]{:S(2)}, u32[]{:S(2)}) async-start(bf16[96,8,288]{0,2,1:T(8,128)(2,1)} %bitcast.11), calls=%async_computation | async-start | bytes 1179648 | tf_op jit(solution)/shard_map/all_to_all | solution.py:81
  62.5 3.5 copy-start.13
  66.0 5.3 %copy-start.29 = (s32[1,128]{1,0:T(1,128)S(1)}, s32[1,128]{1,0:T(1,128)}, u32[]{:S(2)}) copy-start(s32[1,128]{1,0:T(1,128)} %param.16) | copy-start | bytes 1540
  67.0 29.7 %all-to-all-start.1 = ((bf16[8,128,288]{1,2,0:T(8,128)(2,1)}), bf16[8,128,288]{1,2,0:T(8,128)(2,1)S(1)}, u32[]{:S(2)}, u32[]{:S(2)}) async-start(bf16[8,128,288]{1,2,0:T(8,128)(2,1)} %bitcast.124), calls=%async_computation.1 | async-start | bytes 1179648 | tf_op jit(solution)/shard_map/all_to_all | solution.py:81
  70.5 63.5 %all-gather.13.cloned.1.call-start = ((), (), s32[]{:S(2)}) async-start(), calls=%async_computation.21 | async-start | bytes 1769472 | tf_op jit(solution)/shard_map/all_gather | solution.py:143
  71.2 89.0 %all-gather.11.cloned.1.call-start = ((), (), s32[]{:S(2)}) async-start(), calls=%async_computation.20 | async-start | bytes 1769472 | tf_op jit(solution)/shard_map/all_gather | solution.py:155
  96.7 2.1 copy-start.6
  96.7 2.1 copy-start.3
  98.8 3.5 copy-start.11
  100.7 2.4 copy-start.22
  100.9 2.2 copy-start.26
  101.4 6.0 %copy-start.30 = (bf16[384]{0:T(512)(128)(2,1)S(1)}, bf16[384]{0:T(512)(128)(2,1)}, u32[]{:S(2)}) copy-start(bf16[384]{0:T(512)(128)(2,1)} %param.26) | copy-start | bytes 2308
  103.2 33.3 %all-to-all-start.2 = ((bf16[96,8,384]{2,0,1:T(8,128)(2,1)}), bf16[96,8,384]{2,0,1:T(8,128)(2,1)}, u32[]{:S(2)}, u32[]{:S(2)}) async-start(bf16[96,8,384]{2,0,1:T(8,128)(2,1)} %bitcast.123), calls=%async_computation.2 | async-start | bytes 1179648 | tf_op jit(solution)/shard_map/all_to_all | solution.py:81
  107.4 96.4 %reduce-scatter.3.cloned.1.call-start = ((), (), s32[]{:S(2)}) async-start(), calls=%async_computation.22 | async-start | bytes 1769472 | tf_op jit(solution)/shard_map/reduce_scatter | solution.py:165
  166.4 3.4 copy-start.37
  203.8 41.3 %all-to-all-start.3 = ((bf16[8,128,768]{2,1,0:T(8,128)(2,1)}), bf16[8,128,768]{2,1,0:T(8,128)(2,1)S(1)}, u32[]{:S(2)}, u32[]{:S(2)}) async-start(bf16[8,128,768]{2,1,0:T(8,128)(2,1)} %bitcast.139), calls=%async_computation.4 | async-start | bytes 3145728 | tf_op jit(solution)/shard_map/all_to_all | solution.py:81
  207.3 143.6 %all-gather.15.cloned.1.call-start = ((), (), s32[]{:S(2)}) async-start(), calls=%async_computation.24 | async-start | bytes 1769472 | tf_op jit(solution)/shard_map/all_gather | solution.py:177
  245.1 1.8 copy-start.4
  245.4 2.4 copy-start.2
  247.7 123.4 %reduce-scatter.5.cloned.1.call-start = ((), (), s32[]{:S(2)}) async-start(), calls=%async_computation.23 | async-start | bytes 1769472 | tf_op jit(solution)/shard_map/reduce_scatter | solution.py:197
  249.3 2.5 copy-start.9
  249.3 2.9 copy-start.7
  253.1 29.9 %copy-start.14 = (bf16[768,288]{0,1:T(8,128)(2,1)S(1)}, bf16[768,288]{0,1:T(8,128)(2,1)}, u32[]{:S(2)}) copy-start(bf16[768,288]{0,1:T(8,128)(2,1)} %copy-done.13) | copy-start | bytes 1327108
  289.6 12.6 %all-to-all-start.13 = ((bf16[4,192,384]{2,1,0:T(8,128)(2,1)}), bf16[4,192,384]{2,1,0:T(8,128)(2,1)S(1)}, u32[]{:S(2)}, u32[]{:S(2)}) async-start(bf16[4,192,384]{2,1,0:T(8,128)(2,1)} %bitcast.52), calls=%async_computation.15 | async-start | bytes 1179648 | tf_op jit(solution)/shard_map/all_to_all | solution.py:81
  302.2 11.8 %all-to-all-start.12 = ((bf16[4,96,768]{2,1,0:T(8,128)(2,1)}), bf16[4,96,768]{2,1,0:T(8,128)(2,1)S(1)}, u32[]{:S(2)}, u32[]{:S(2)}) async-start(bf16[4,96,768]{2,1,0:T(8,128)(2,1)} %bitcast.49), calls=%async_computation.14 | async-start | bytes 1179648 | tf_op jit(solution)/shard_map/all_to_all | solution.py:81
  314.0 10.3 %all-to-all-start.14 = ((bf16[8,24,384]{2,1,0:T(8,128)(2,1)}), bf16[8,24,384]{2,1,0:T(8,128)(2,1)S(1)}, u32[]{:S(2)}, u32[]{:S(2)}) async-start(bf16[8,24,384]{2,1,0:T(8,128)(2,1)} %bitcast.53), calls=%async_computation.16 | async-start | bytes 294912 | tf_op jit(solution)/shard_map/all_to_all | solution.py:81
  335.9 11.7 %all-to-all-start.7 = ((bf16[128,8,96]{0,2,1:T(8,128)(2,1)}), bf16[128,8,96]{0,2,1:T(8,128)(2,1)S(1)}, u32[]{:S(2)}, u32[]{:S(2)}) async-start(bf16[128,8,96]{0,2,1:T(8,128)(2,1)} %bitcast.40), calls=%async_computation.9 | async-start | bytes 393216 | tf_op jit(solution)/shard_map/all_to_all | solution.py:81
  340.3 21.0 %copy-start.19 = (f32[768]{0:T(1024)S(1)}, f32[768]{0:T(1024)}, u32[]{:S(2)}) copy-start(f32[768]{0:T(1024)} %get-tuple-element.24) | copy-start | bytes 9220
  340.3 21.1 %copy-start.18 = (f32[768]{0:T(1024)S(1)}, f32[768]{0:T(1024)}, u32[]{:S(2)}) copy-start(f32[768]{0:T(1024)} %get-tuple-element.30) | copy-start | bytes 9220
  340.3 21.2 %copy-start.16 = (f32[12,64]{1,0:T(8,128)S(1)}, f32[12,64]{1,0:T(8,128)}, u32[]{:S(2)}) copy-start(f32[12,64]{1,0:T(8,128)} %get-tuple-element.51) | copy-start | bytes 9220
  340.3 21.3 %copy-start.15 = (f32[12,64]{1,0:T(8,128)S(1)}, f32[12,64]{1,0:T(8,128)}, u32[]{:S(2)}) copy-start(f32[12,64]{1,0:T(8,128)} %get-tuple-element.53) | copy-start | bytes 9220
  347.6 10.3 %all-to-all-start.10 = ((bf16[8,24,288]{2,1,0:T(8,128)(2,1)}), bf16[8,24,288]{2,1,0:T(8,128)(2,1)S(1)}, u32[]{:S(2)}, u32[]{:S(2)}) async-start(bf16[8,24,288]{2,1,0:T(8,128)(2,1)} %bitcast.46), calls=%async_computation.12 | async-start | bytes 294912 | tf_op jit(solution)/shard_map/all_to_all | solution.py:81
  357.9 8.4 %all-to-all-start.8 = ((bf16[4,24,768]{2,1,0:T(8,128)(2,1)}), bf16[4,24,768]{2,1,0:T(8,128)(2,1)S(1)}, u32[]{:S(2)}, u32[]{:S(2)}) async-start(bf16[4,24,768]{2,1,0:T(8,128)(2,1)} %bitcast.42), calls=%async_computation.10 | async-start | bytes 294912 | tf_op jit(solution)/shard_map/all_to_all | solution.py:81
  367.4 3.8 copy-start.21
  367.4 5.0 %copy-start.32 = (f32[128]{0:T(128)S(1)}, f32[128]{0:T(128)}, u32[]{:S(2)}) copy-start(f32[128]{0:T(128)} %copy-done.31) | copy-start | bytes 1540
  367.4 5.0 %copy-start.25 = (f32[128]{0:T(128)S(1)}, f32[128]{0:T(128)}, u32[]{:S(2)}) copy-start(f32[128]{0:T(128)} %copy-done.24) | copy-start | bytes 1540
  367.4 6.3 %copy-start.5 = (bf16[128,768]{1,0:T(8,128)(2,1)S(1)}, bf16[128,768]{1,0:T(8,128)(2,1)}, u32[]{:S(2)}) copy-start(bf16[128,768]{1,0:T(8,128)(2,1)} %param.29) | copy-start | bytes 589828
  367.4 17.4 %all-to-all-start.15 = ((bf16[4,192,768]{2,1,0:T(8,128)(2,1)}), bf16[4,192,768]{2,1,0:T(8,128)(2,1)S(1)}, u32[]{:S(2)}, u32[]{:S(2)}) async-start(bf16[4,192,768]{2,1,0:T(8,128)(2,1)} %broadcast_in_dim.73), calls=%async_computation.17 | async-start | bytes 2359296 | tf_op jit(solution)/shard_map/all_to_all | solution.py:81
  373.7 24.5 %copy-start.28 = (f32[384]{0:T(512)S(1)}, f32[384]{0:T(512)}, u32[]{:S(2)}) copy-start(f32[384]{0:T(512)} %get-tuple-element.41) | copy-start | bytes 4612
  384.8 9.1 %all-to-all-start.5 = ((f32[8,1,768]{2,1,0:T(1,128)}), f32[8,1,768]{2,1,0:T(1,128)S(1)}, u32[]{:S(2)}, u32[]{:S(2)}) async-start(f32[8,1,768]{2,1,0:T(1,128)} %all_to_all.158), calls=%async_computation.7 | async-start | bytes 49152 | tf_op jit(solution)/shard_map/all_to_all | solution.py:81
  394.7 12.4 %all-to-all-start.11 = ((bf16[4,96,768]{2,1,0:T(8,128)(2,1)}), bf16[4,96,768]{2,1,0:T(8,128)(2,1)S(1)}, u32[]{:S(2)}, u32[]{:S(2)}) async-start(bf16[4,96,768]{2,1,0:T(8,128)(2,1)} %broadcast_in_dim.72), calls=%async_computation.13 | async-start | bytes 1179648 | tf_op jit(solution)/shard_map/all_to_all | solution.py:81
  407.7 8.6 %all-to-all-start.6 = ((f32[4,1,1152]{2,1,0:T(1,128)}), f32[4,1,1152]{2,1,0:T(1,128)}, u32[]{:S(2)}, u32[]{:S(2)}) async-start(f32[4,1,1152]{2,1,0:T(1,128)} %broadcast_in_dim.39), calls=%async_computation.8 | async-start | bytes 36864 | tf_op jit(solution)/shard_map/all_to_all | solution.py:81
  (11 other events, 9.8 us)
Sparse Core Ops, SparseCore 0:
  27.8 36.0 all-gather.6
  65.6 31.9 all-gather.8
  99.3 34.7 all-gather.12
  136.1 24.1 all-gather.10
  169.9 33.8 reduce-scatter.2
  247.8 34.9 all-gather.14
  285.3 33.2 reduce-scatter.4

commit v3 on v2

--- a/solution.py
+++ b/solution.py
@@ -79,12 +79,6 @@
 
 def exchange(field, axis, split, concat):
     return lax.all_to_all(field, axis, split_axis=split, concat_axis=concat, tiled=True)
-
-
-def sum_exchanged(field, axis):
-    parts = lax.axis_size(axis)
-    blocks = exchange(field.reshape((parts, -1) + field.shape[1:]), axis, 0, 0)
-    return jnp.sum(blocks.astype(jnp.float32), axis=0)
 
 
 def spread(field, axis):
@@ -129,23 +123,16 @@
     gain_one, shift_one, q_bias, v_bias, proj_bias_full, gain_two, shift_two, out_bias_full = (
         small_full[i] for i in range(8)
     )
+    qkv_full = lax.all_gather(qkv_weight, "shard", axis=0, tiled=True)
     proj_full = lax.all_gather(proj_weight, "shard", axis=0, tiled=True)
-    qkv_cols = exchange(qkv_weight, "shard", 1, 0)
     fc_cols = exchange(fc_weight, "shard", 1, 0)
-    qkv_bias = jnp.concatenate([q_bias, jnp.zeros_like(q_bias), v_bias])
-    width = qkv_cols.shape[1]
-    bias_cols = lax.dynamic_slice_in_dim(qkv_bias, lax.axis_index("shard") * width, width)
-
     inputs = tokens.astype(jnp.float32)
     normed_f, first_back = jax.vjp(layer_norm, inputs, gain_one, shift_one)
-    first_all = lax.all_gather(normed_f.astype(low), "shard", axis=0, tiled=True)
-    cot_later, first_all = lax.optimization_barrier((cotangent, first_all))
-    cot_all = lax.all_gather(cot_later, "shard", axis=0, tiled=True)
-    projected_cols = jnp.dot(first_all, qkv_cols, preferred_element_type=jnp.float32) + bias_cols
-    projected = exchange(projected_cols.astype(low), "shard", 0, 1)
-    query = projected[:, :D]
-    keys = projected[:, D : 2 * D]
-    values = projected[:, 2 * D :]
+    normed_first = normed_f.astype(low)
+    projected = jnp.dot(normed_first, qkv_full, preferred_element_type=jnp.float32)
+    query = (projected[:, :D] + q_bias).astype(low)
+    keys = projected[:, D : 2 * D].astype(low)
+    values = (projected[:, 2 * D :] + v_bias).astype(low)
     attended, logsum = attend_forward(query, keys, values, segments)
     residual = (
         inputs + jnp.dot(attended, proj_full, preferred_element_type=jnp.float32) + proj_bias_full
@@ -153,6 +140,8 @@
     cot_f = cotangent.astype(jnp.float32)
     normed_s, second_back = jax.vjp(layer_norm, residual, gain_two, shift_two)
     normed_all = lax.all_gather(normed_s.astype(low), "shard", axis=0, tiled=True)
+    cot_later, normed_all = lax.optimization_barrier((cotangent, normed_all))
+    cot_all = lax.all_gather(cot_later, "shard", axis=0, tiled=True)
     pre_act = jnp.dot(normed_all, fc_cols, preferred_element_type=jnp.float32) + fc_bias.astype(
         jnp.float32
     )
@@ -166,9 +155,18 @@
     term_out_weight = jnp.dot(hidden.T, cot_all, preferred_element_type=jnp.float32) * factor
     term_fc_weight = jnp.dot(normed_all.T, grad_pre_low, preferred_element_type=jnp.float32) * factor
     out_part = jnp.dot(hidden, out_weight, preferred_element_type=jnp.float32).astype(low)
-    out_part, attended_later, grad_normed_low = lax.optimization_barrier(
-        (out_part, attended, grad_normed_low)
-    )
+    ff_terms = jnp.concatenate(
+        [
+            term_out_weight.astype(low).reshape(reps, -1, D),
+            by_replica(term_fc_weight.astype(low), shards, reps).reshape(reps, -1, D),
+        ],
+        axis=1,
+    )
+    ff_sum = jnp.sum(exchange(ff_terms, "rep", 0, 0).astype(jnp.float32), axis=0).astype(low)
+    first_later, attended_later, grad_normed_low, ff_sum = lax.optimization_barrier(
+        (normed_first, attended, grad_normed_low, ff_sum)
+    )
+    first_all = lax.all_gather(first_later, "shard", axis=0, tiled=True)
     grad_normed_second = grad_normed_low.astype(jnp.float32)
 
     grad_from_norm, second_gain_sum, second_shift_sum = second_back(grad_normed_second)
@@ -179,35 +177,43 @@
     grad_attended = jnp.dot(
         grad_residual_low, proj_full.T, preferred_element_type=jnp.float32
     ).astype(low)
-    result = (residual + sum_exchanged(out_part, "shard") + out_bias_full).astype(low)
-    out_piece = sum_exchanged(term_out_weight.astype(low), "rep").astype(low)
-    fc_piece = sum_exchanged(by_replica(term_fc_weight.astype(low), shards, reps), "rep").astype(low)
+    out_rows = out_weight.shape[0] // reps
+    out_piece = ff_sum[:out_rows]
+    fc_piece = ff_sum[out_rows:].reshape(D // reps, -1)
     fc_piece = exchange(fc_piece, "shard", 0, 1)
     ff_all = spread(jnp.concatenate([out_piece, fc_piece.reshape(-1, D)]), "rep").astype(jnp.float32)
-    out_rows = out_piece.shape[0]
+
+    grad_query, grad_keys, grad_values = attend_backward(
+        query, keys, values, segments, attended, logsum, grad_attended
+    )
+    grad_projected = jnp.concatenate([grad_query, grad_keys, grad_values], axis=1).astype(low)
+    grad_projected, ff_all = lax.optimization_barrier((grad_projected, ff_all))
     out_grad = ff_all[:, :out_rows].reshape(-1, D)
     fc_grad = ff_all[:, out_rows:].reshape(-1, FF)
-
-    grad_query, grad_keys, grad_values = attend_backward(
-        query, keys, values, segments, attended, logsum, grad_attended
-    )
-    grad_projected = jnp.concatenate([grad_query, grad_keys, grad_values], axis=1).astype(low)
     grad_cols = exchange(grad_projected, "shard", 1, 0)
-    grad_first_part = jnp.dot(grad_cols, qkv_cols.T, preferred_element_type=jnp.float32).astype(low)
-    grad_normed_first = lax.psum_scatter(
-        grad_first_part, "shard", scatter_dimension=0, tiled=True
-    ).astype(jnp.float32)
+    grad_normed_first = jnp.dot(grad_projected, qkv_full.T, preferred_element_type=jnp.float32)
+    out_later, grad_cols = lax.optimization_barrier((out_part, grad_cols))
+    out_sum = lax.psum_scatter(out_later, "shard", scatter_dimension=0, tiled=True)
+    result = (residual + out_sum.astype(jnp.float32) + out_bias_full).astype(low)
     term_qkv_weight = jnp.dot(first_all.T, grad_cols, preferred_element_type=jnp.float32) * factor
     term_proj_weight = (
         jnp.dot(attended_cols.T, grad_residual_all, preferred_element_type=jnp.float32) * factor
     )
-    proj_piece = sum_exchanged(term_proj_weight.astype(low), "rep").astype(low)
-    qkv_piece = sum_exchanged(by_replica(term_qkv_weight.astype(low), shards, reps), "rep").astype(low)
+    attn_terms = jnp.concatenate(
+        [
+            term_proj_weight.astype(low).reshape(reps, -1, D),
+            by_replica(term_qkv_weight.astype(low), shards, reps).reshape(reps, -1, D),
+        ],
+        axis=1,
+    )
+    attn_sum = jnp.sum(exchange(attn_terms, "rep", 0, 0).astype(jnp.float32), axis=0).astype(low)
+    proj_rows = proj_weight.shape[0] // reps
+    proj_piece = attn_sum[:proj_rows]
+    qkv_piece = attn_sum[proj_rows:].reshape(D // reps, -1)
     qkv_piece = exchange(qkv_piece, "shard", 0, 1)
     attn_all = spread(jnp.concatenate([proj_piece, qkv_piece.reshape(-1, D)]), "rep").astype(
         jnp.float32
     )
-    proj_rows = proj_piece.shape[0]
     proj_grad = attn_all[:, :proj_rows].reshape(-1, D)
     qkv_grad = attn_all[:, proj_rows:].reshape(-1, 3 * D)
 

time: 428 us -> 347 us (0.81)
  waiting for transfers between devices: 229 us -> 158 us
  blocking collectives: 54.8 us -> 33.9 us
  local copies, waits for them, and re-layouts: 21.6 us -> 40.4 us
  starting transfers between devices: 50.1 us -> 40.7 us
    all_to_all x14 -> x10, waiting for transfers between devices: 145 us -> 48.6 us  [exchange(): lax.all_to_all(field, axis, split_axis=split, concat_axis=concat, tiled=T...]
    reduce_scatter x1, waiting for transfers between devices: 31.6 us -> 7.81 us  [per_device(): lax.psum_scatter(grad_normed_part, 'shard', scatter_dimension=0, tiled=True)]
    all_gather x1 -> x2, waiting for transfers between devices: 1.43 us -> 25.1 us  [the longest x1 25.1 us: per_device(): qkv_full = lax.all_gather(qkv_weight, 'shard', axis=0, tiled=True)]
    all_to_all x2 -> x1, blocking collectives: 40.4 us -> 19.4 us  [exchange(): lax.all_to_all(field, axis, split_axis=split, concat_axis=concat, tiled=T...]
    all_gather x1, waiting for transfers between devices: 0.01 us -> 19.2 us  [per_device(): proj_full = lax.all_gather(proj_weight, 'shard', axis=0, tiled=True)]
    all_to_all x14 -> x10, starting transfers between devices: 49.8 us -> 40.4 us  [exchange(): lax.all_to_all(field, axis, split_axis=split, concat_axis=concat, tiled=T...]
    all_to_all x7, local copies, waits for them, and re-layouts: 3.22 us -> 8.92 us  [exchange(): lax.all_to_all(field, axis, split_axis=split, concat_axis=concat, tiled=T...]
    another operation x9, local copies, waits for them, and re-layouts: 0.69 us -> 5.8 us  [per_device(): jnp.stack([first_gain_sum, first_shift_sum, jnp.sum(grad_query, axis=0),...]
  transfers between devices with their start and end apart: 21 -> 18, of which waited for: 17 -> 13; matrix products, arithmetic and copies ran while one was open for 12% -> 23% of each run, Pallas kernels for 0% -> 0%
where the time goes in v3:
time: 347 us; the launch traced here: 346 us
  waiting for transfers between devices  158 us (46%)
  starting transfers between devices  40.7 us (12%)
  local copies, waits for them, and re-layouts  40.4 us (12%)
  matrix products  39.6 us (11%)
  blocking collectives  33.9 us (10%)
  other arithmetic  18.2 us (5%)
  between operations  14.9 us (4%)
    all_to_all x10, waiting for transfers between devices, exchange(): lax.all_to_all(field, axis, split_axis=split, concat_axis=concat, tiled=T...  48.6 us
    all_to_all x10, starting transfers between devices, exchange(): lax.all_to_all(field, axis, split_axis=split, concat_axis=concat, tiled=T...  40.4 us
    all_gather x1, waiting for transfers between devices, per_device(): cot_all = lax.all_gather(cot_later, 'shard', axis=0, tiled=True)  30.8 us
    all_gather x1, waiting for transfers between devices, per_device(): qkv_full = lax.all_gather(qkv_weight, 'shard', axis=0, tiled=True)  25.1 us
    all_gather x1, waiting for transfers between devices, per_device(): lax.all_gather(normed_s.astype(low), 'shard', axis=0, tiled=True)  24.9 us
    all_to_all x1, blocking collectives, exchange(): lax.all_to_all(field, axis, split_axis=split, concat_axis=concat, tiled=T...  19.4 us
    all_gather x1, waiting for transfers between devices, per_device(): proj_full = lax.all_gather(proj_weight, 'shard', axis=0, tiled=True)  19.2 us
    all_gather x1, blocking collectives, per_device(): lax.all_gather(small, 'shard', axis=1, tiled=True).astype(jnp.float32)  14.5 us
  transfers between devices with their start and end apart: 18, of which 13 were waited for; matrix products, arithmetic and copies ran while one was open for 23% of the time, Pallas kernels for 0%

profile of v3, /device:TPU:0, one launch (start us, length us, event | category | flops | bytes accessed | tf_op | source)
XLA Modules:
  0.0 345.6 jit_solution(11735301634824392414)
XLA Ops:
  11.7 14.5 %all-gather = bf16[8,96,8]{1,2,0:T(8,128)(2,1)S(1)} all-gather(bf16[1,96,8]{1,2,0:T(8,128)(2,1)S(1)} %bitcast.133), channel_id=1, replica_groups=mesh['rep'=4,'shard'=8] {'shard'}, dimensions={0}, use_global_device_ids=true | all-gather | bytes 13824 | tf_op jit(solution)/shard_map/all_gather | solution.py:122
  28.9 25.1 %all-gather.8.cloned.1.call-done = bf16[768,2304]{1,0:T(8,128)(2,1)} async-done(((bf16[96,2304]{1,0:T(8,128)(2,1)}), bf16[768,2304]{1,0:T(8,128)(2,1)}) %all-gather.8.cloned.1.call-update) | async-done | bytes 3538960 | tf_op jit(solution)/shard_map/all_gather | solution.py:126
  53.9 2.6 fusion.57
  58.0 19.2 %all-gather.10.cloned.1.call-done = bf16[768,768]{1,0:T(8,128)(2,1)} async-done(((bf16[96,768]{1,0:T(8,128)(2,1)}), bf16[768,768]{1,0:T(8,128)(2,1)}) %all-gather.10.cloned.1.call-update) | async-done | bytes 1179664 | tf_op jit(solution)/shard_map/all_gather | solution.py:127
  77.2 1.8 fusion.56
  80.6 24.9 %all-gather.12.cloned.1.call-done = bf16[1024,768]{1,0:T(8,128)(2,1)} async-done(((bf16[128,768]{1,0:T(8,128)(2,1)}), bf16[1024,768]{1,0:T(8,128)(2,1)}) %all-gather.12.cloned.1.call-update) | async-done | bytes 1572880 | tf_op jit(solution)/shard_map/all_gather | solution.py:142
  106.4 3.5 %all-to-all-start = ((bf16[96,8,384]{2,0,1:T(8,128)(2,1)}), bf16[96,8,384]{2,0,1:T(8,128)(2,1)S(1)}, u32[]{:S(2)}, u32[]{:S(2)}) async-start(bf16[96,8,384]{2,0,1:T(8,128)(2,1)} %bitcast.106), calls=%async_computation | async-start | bytes 1179648 | tf_op jit(solution)/shard_map/all_to_all | solution.py:81
  110.0 30.8 %all-gather.14.cloned.1.call-done = bf16[1024,768]{1,0:T(8,128)(2,1)} async-done(((bf16[128,768]{1,0:T(8,128)(2,1)}), bf16[1024,768]{1,0:T(8,128)(2,1)}) %all-gather.14.cloned.1.call-update) | async-done | bytes 1572880 | tf_op jit(solution)/shard_map/all_gather | solution.py:144
  140.8 3.6 %fusion.58 = f32[1024,384]{1,0:T(8,128)} fusion(bf16[1024,768]{1,0:T(8,128)(2,1)} %all-gather.14.cloned.1.call-done, bf16[384,768]{1,0:T(8,128)(2,1)S(1)} %copy-done), kind=kOutput, calls=%fused_computation.119 | convolution fusion | flops 603979776 | bytes 3735552 | tf_op jit(solution)/shard_map/dot_general | solution.py:150
  144.4 5.6 %fusion.47 = (f32[384]{0:T(512)}, bf16[1024,384]{1,0:T(8,128)(2,1)S(1)}, f32[1024,384]{1,0:T(8,128)}) fusion(f32[1024,384]{1,0:T(8,128)} %fusion.58, f32[384]{0:T(512)S(1)} %convert_element_type.103, bf16[1024,768]{1,0:T(8,128)(2,1)} %all-gather.12.cloned.1.call-done, bf16[768,384]{1,0:T(8,128)(2,1)S(1)} %bitcast.125), kind=kOutput, calls=%fused_computation.109 | convolution fusion | flops 612630144 | bytes 6097920 | tf_op jit(solution)/shard_map/dot_general | solution.py:145
  150.9 2.2 convolution_convert_fusion
  153.1 2.6 fusion.7
  156.0 2.8 fusion.6
  158.9 19.4 %all_to_all.125 = bf16[4,192,768]{2,1,0:T(8,128)(2,1)S(1)} all-to-all(bf16[4,192,768]{2,1,0:T(8,128)(2,1)S(1)} %pad_maximum_fusion), channel_id=1, replica_groups=mesh['rep'=4,'shard'=8] {'rep'}, dimensions={0} | all-to-all | bytes 2359296 | tf_op jit(solution)/shard_map/all_to_all | solution.py:81
  179.2 7.8 %reduce-scatter.3.cloned.1.call-done = bf16[128,768]{1,0:T(8,128)(2,1)} async-done(((bf16[1024,768]{1,0:T(8,128)(2,1)}), bf16[128,768]{1,0:T(8,128)(2,1)}) %reduce-scatter.3.cloned.1.call-update) | async-done | bytes 196624 | tf_op jit(solution)/shard_map/reduce_scatter | solution.py:154
  187.1 1.7 fusion.53
  188.8 1.7 all_to_all.93
  190.5 4.0 %all-to-all-start.2 = ((bf16[8,24,384]{2,1,0:T(8,128)(2,1)}), bf16[8,24,384]{2,1,0:T(8,128)(2,1)}, u32[]{:S(2)}, u32[]{:S(2)}) async-start(bf16[8,24,384]{2,1,0:T(8,128)(2,1)} %all_to_all.93), calls=%async_computation.3 | async-start | bytes 294912 | tf_op jit(solution)/shard_map/all_to_all | solution.py:81
  194.6 1.8 fusion.30
  199.8 2.1 convolution_convert_fusion.3
  203.6 1.9 all-to-all-done.2
  207.6 4.6 %all-to-all-start.3 = ((bf16[4,192,768]{2,1,0:T(8,128)(2,1)}), bf16[4,192,768]{2,1,0:T(8,128)(2,1)}, u32[]{:S(2)}, u32[]{:S(2)}) async-start(bf16[4,192,768]{2,1,0:T(8,128)(2,1)} %broadcast_in_dim.34), calls=%async_computation.4 | async-start | bytes 2359296 | tf_op jit(solution)/shard_map/all_to_all | solution.py:81
  215.4 11.7 %all-to-all-done.3 = bf16[4,192,768]{2,1,0:T(8,128)(2,1)} async-done(((bf16[4,192,768]{2,1,0:T(8,128)(2,1)}), bf16[4,192,768]{2,1,0:T(8,128)(2,1)}, u32[]{:S(2)}, u32[]{:S(2)}) %all-to-all-start.3) | async-done | bytes 1179680 | tf_op jit(solution)/shard_map/all_to_all | solution.py:81
  227.1 1.5 convert_element_type.115
  228.6 4.2 %all-to-all-start.4 = ((bf16[128,8,288]{0,2,1:T(8,128)(2,1)}), bf16[128,8,288]{0,2,1:T(8,128)(2,1)}, u32[]{:S(2)}, u32[]{:S(2)}) async-start(bf16[128,8,288]{0,2,1:T(8,128)(2,1)} %bitcast.107), calls=%async_computation.5 | async-start | bytes 1179648 | tf_op jit(solution)/shard_map/all_to_all | solution.py:81
  232.8 3.8 %convolution_convert_fusion.1 = bf16[1024,768]{1,0:T(8,128)(2,1)} fusion(bf16[384,768]{1,0:T(8,128)(2,1)S(1)} %copy-done, f32[1024,384]{1,0:T(8,128)} %get-tuple-element.76), kind=kOutput, calls=%fused_computation.3 | convolution fusion | flops 608305152 | bytes 3735552 | tf_op jit(solution)/shard_map/dot_general | solution.py:157
  240.7 12.3 %all-to-all-done.4 = bf16[128,8,288]{0,2,1:T(8,128)(2,1)} async-done(((bf16[128,8,288]{0,2,1:T(8,128)(2,1)}), bf16[128,8,288]{0,2,1:T(8,128)(2,1)}, u32[]{:S(2)}, u32[]{:S(2)}) %all-to-all-start.4) | async-done | bytes 589856 | tf_op jit(solution)/shard_map/all_to_all | solution.py:81
  253.0 4.2 %all-to-all-start.7 = ((bf16[128,8,96]{0,2,1:T(8,128)(2,1)}), bf16[128,8,96]{0,2,1:T(8,128)(2,1)}, u32[]{:S(2)}, u32[]{:S(2)}) async-start(bf16[128,8,96]{0,2,1:T(8,128)(2,1)} %bitcast.109), calls=%async_computation.9 | async-start | bytes 393216 | tf_op jit(solution)/shard_map/all_to_all | solution.py:81
  257.2 2.0 copy_bitcast_fusion
  259.3 4.2 %fusion.46 = (f32[768]{0:T(1024)}, f32[128]{0:T(128)S(1)}, f32[128,768]{1,0:T(8,128)S(1)}) fusion(f32[768]{0:T(1024)S(1)} %get-tuple-element.50, f32[128]{0:T(128)S(1)} %copy-done.20, bf16[128,768]{1,0:T(8,128)(2,1)S(1)} %copy-done.1, bf16[128,2304]{0,1:T(8,128)(2,1)} %pad_maximum_fusion.1, bf16[768,2304]{1,0:T(8,128)(2,1)} %all-gather.8.cloned.1.call-done), kind=kOutput, calls=%fused_computation.108 | convolution fusion | flops 453573760 | bytes 4725760 | tf_op jit(solution)/shard_map/dot_general | solution.py:194
  267.3 3.0 fusion.11
  270.3 2.1 copy.150
  272.4 1.9 copy.151
  274.4 2.8 reshape_reshape.7
  277.1 5.0 %all-to-all-start.5 = ((f32[8,1,768]{2,1,0:T(1,128)}), f32[8,1,768]{2,1,0:T(1,128)S(1)}, u32[]{:S(2)}, u32[]{:S(2)}) async-start(f32[8,1,768]{2,1,0:T(1,128)} %all_to_all.113), calls=%async_computation.7 | async-start | bytes 49152 | tf_op jit(solution)/shard_map/all_to_all | solution.py:81
  282.1 2.0 fusion.14
  285.0 3.0 all-to-all-done.5
  288.0 4.2 %all-to-all-start.8 = ((bf16[4,96,768]{2,1,0:T(8,128)(2,1)}), bf16[4,96,768]{2,1,0:T(8,128)(2,1)}, u32[]{:S(2)}, u32[]{:S(2)}) async-start(bf16[4,96,768]{2,1,0:T(8,128)(2,1)} %pad_maximum_fusion.2), calls=%async_computation.10 | async-start | bytes 1179648 | tf_op jit(solution)/shard_map/all_to_all | solution.py:81
  292.3 9.2 %all-to-all-done.8 = bf16[4,96,768]{2,1,0:T(8,128)(2,1)} async-done(((bf16[4,96,768]{2,1,0:T(8,128)(2,1)}), bf16[4,96,768]{2,1,0:T(8,128)(2,1)}, u32[]{:S(2)}, u32[]{:S(2)}) %all-to-all-start.8) | async-done | bytes 589856 | tf_op jit(solution)/shard_map/all_to_all | solution.py:81
  302.1 3.3 all-to-all-start.6
  307.1 1.8 all_to_all.109
  310.0 4.0 %all-to-all-start.9 = ((bf16[8,24,288]{2,1,0:T(8,128)(2,1)}), bf16[8,24,288]{2,1,0:T(8,128)(2,1)}, u32[]{:S(2)}, u32[]{:S(2)}) async-start(bf16[8,24,288]{2,1,0:T(8,128)(2,1)} %all_to_all.109), calls=%async_computation.11 | async-start | bytes 294912 | tf_op jit(solution)/shard_map/all_to_all | solution.py:81
  314.0 1.7 fusion.50
  315.7 2.5 reshape.296
  318.3 2.8 all-to-all-done.9
  323.1 3.5 %all-to-all-start.10 = ((bf16[4,96,768]{2,1,0:T(8,128)(2,1)}), bf16[4,96,768]{2,1,0:T(8,128)(2,1)S(1)}, u32[]{:S(2)}, u32[]{:S(2)}) async-start(bf16[4,96,768]{2,1,0:T(8,128)(2,1)} %broadcast_in_dim.68), calls=%async_computation.12 | async-start | bytes 1179648 | tf_op jit(solution)/shard_map/all_to_all | solution.py:81
  328.5 6.6 %all-to-all-done.10 = bf16[4,96,768]{2,1,0:T(8,128)(2,1)S(1)} async-done(((bf16[4,96,768]{2,1,0:T(8,128)(2,1)}), bf16[4,96,768]{2,1,0:T(8,128)(2,1)S(1)}, u32[]{:S(2)}, u32[]{:S(2)}) %all-to-all-start.10) | async-done | bytes 589856 | tf_op jit(solution)/shard_map/all_to_all | solution.py:81
  337.1 1.7 add_convert_fusion
  (168 shorter events, 41.7 us)
Async XLA Ops:
  7.2 133.6 %copy-start = (bf16[384,768]{1,0:T(8,128)(2,1)S(1)}, bf16[384,768]{1,0:T(8,128)(2,1)}, u32[]{:S(2)}) copy-start(bf16[384,768]{1,0:T(8,128)(2,1)} %param.27) | copy-start | bytes 1769476
  7.2 46.7 %all-gather.8.cloned.1.call-start = ((), (), s32[]{:S(2)}) async-start(), calls=%async_computation.13 | async-start | bytes 3981312 | tf_op jit(solution)/shard_map/all_gather | solution.py:126
  7.9 69.2 %all-gather.10.cloned.1.call-start = ((), (), s32[]{:S(2)}) async-start(), calls=%async_computation.14 | async-start | bytes 1327104 | tf_op jit(solution)/shard_map/all_gather | solution.py:127
  8.7 96.8 %all-gather.12.cloned.1.call-start = ((), (), s32[]{:S(2)}) async-start(), calls=%async_computation.15 | async-start | bytes 1769472 | tf_op jit(solution)/shard_map/all_gather | solution.py:142
  9.8 46.8 %copy-start.19 = (f32[128]{0:T(128)}, f32[128]{0:T(128)S(1)}, u32[]{:S(2)}) copy-start(f32[128]{0:T(128)S(1)} %broadcast_multiply_fusion.2) | copy-start | bytes 1540
  10.9 45.7 %copy-start.23 = (f32[128]{0:T(128)}, f32[128]{0:T(128)S(1)}, u32[]{:S(2)}) copy-start(f32[128]{0:T(128)S(1)} %fusion.41) | copy-start | bytes 1540
  28.9 27.7 %copy-start.6 = (bf16[128,768]{1,0:T(8,128)(2,1)}, bf16[128,768]{1,0:T(8,128)(2,1)S(1)}, u32[]{:S(2)}) copy-start(bf16[128,768]{1,0:T(8,128)(2,1)S(1)} %fusion.25) | copy-start | bytes 589828
  56.9 1.1 copy-start.9
  57.1 0.9 copy-start.7
  57.2 19.9 %copy-start.1 = (bf16[128,768]{1,0:T(8,128)(2,1)S(1)}, bf16[128,768]{1,0:T(8,128)(2,1)}, u32[]{:S(2)}) copy-start(bf16[128,768]{1,0:T(8,128)(2,1)} %param.15) | copy-start | bytes 589828
  58.0 145.1 %copy-start.5 = (bf16[12,64,128]{2,1,0:T(8,128)(2,1)}, bf16[12,64,128]{2,1,0:T(8,128)(2,1)S(1)}, u32[]{:S(2)}) copy-start(bf16[12,64,128]{2,1,0:T(8,128)(2,1)S(1)} %convolution_convert_fusion.4) | copy-start | bytes 589828
  77.2 28.4 %copy-start.14 = (bf16[96,3072]{1,0:T(8,128)(2,1)S(1)}, bf16[96,3072]{1,0:T(8,128)(2,1)}, u32[]{:S(2)}) copy-start(bf16[96,3072]{1,0:T(8,128)(2,1)} %param.25) | copy-start | bytes 1769476
  78.9 27.5 %copy-start.22 = (f32[128]{0:T(128)}, f32[128]{0:T(128)S(1)}, u32[]{:S(2)}) copy-start(f32[128]{0:T(128)S(1)} %broadcast_multiply_fusion.1) | copy-start | bytes 1540
  79.2 27.2 %copy-start.25 = (f32[128]{0:T(128)}, f32[128]{0:T(128)S(1)}, u32[]{:S(2)}) copy-start(f32[128]{0:T(128)S(1)} %fusion.42) | copy-start | bytes 1540
  79.7 30.3 %copy-start.29 = (bf16[384]{0:T(512)(128)(2,1)S(1)}, bf16[384]{0:T(512)(128)(2,1)}, u32[]{:S(2)}) copy-start(bf16[384]{0:T(512)(128)(2,1)} %param.26) | copy-start | bytes 2308
  80.5 60.3 %all-gather.14.cloned.1.call-start = ((), (), s32[]{:S(2)}) async-start(), calls=%async_computation.16 | async-start | bytes 1769472 | tf_op jit(solution)/shard_map/all_gather | solution.py:144
  106.4 38.0 %all-to-all-start = ((bf16[96,8,384]{2,0,1:T(8,128)(2,1)}), bf16[96,8,384]{2,0,1:T(8,128)(2,1)S(1)}, u32[]{:S(2)}, u32[]{:S(2)}) async-start(bf16[96,8,384]{2,0,1:T(8,128)(2,1)} %bitcast.106), calls=%async_computation | async-start | bytes 1179648 | tf_op jit(solution)/shard_map/all_to_all | solution.py:81
  110.0 77.1 %reduce-scatter.3.cloned.1.call-start = ((), (), s32[]{:S(2)}) async-start(), calls=%async_computation.17 | async-start | bytes 1769472 | tf_op jit(solution)/shard_map/reduce_scatter | solution.py:154
  150.0 0.9 copy-start.33
  153.1 114.3 %all-gather.18.cloned.1.call-start = ((), (), s32[]{:S(2)}) async-start(), calls=%async_computation.20 | async-start | bytes 1769472 | tf_op jit(solution)/shard_map/all_gather | solution.py:169
  188.8 11.0 %copy-start.2 = (bf16[768,768]{1,0:T(8,128)(2,1)S(1)}, bf16[768,768]{1,0:T(8,128)(2,1)}, u32[]{:S(2)}) copy-start(bf16[768,768]{1,0:T(8,128)(2,1)} %all-gather.10.cloned.1.call-done) | copy-start | bytes 3538948
  190.5 14.9 %all-to-all-start.2 = ((bf16[8,24,384]{2,1,0:T(8,128)(2,1)}), bf16[8,24,384]{2,1,0:T(8,128)(2,1)}, u32[]{:S(2)}, u32[]{:S(2)}) async-start(bf16[8,24,384]{2,1,0:T(8,128)(2,1)} %all_to_all.93), calls=%async_computation.3 | async-start | bytes 294912 | tf_op jit(solution)/shard_map/all_to_all | solution.py:81
  194.5 87.6 %all-gather.16.cloned.1.call-start = ((), (), s32[]{:S(2)}) async-start(), calls=%async_computation.19 | async-start | bytes 1769472 | tf_op jit(solution)/shard_map/all_gather | solution.py:175
  194.6 4.4 %copy-start.12 = (bf16[128,768]{1,0:T(8,128)(2,1)S(1)}, bf16[128,768]{1,0:T(8,128)(2,1)}, u32[]{:S(2)}) copy-start(bf16[128,768]{1,0:T(8,128)(2,1)} %param.29) | copy-start | bytes 589828
  202.0 4.5 %copy-start.15 = (bf16[96,768]{1,0:T(8,128)(2,1)S(1)}, bf16[96,768]{1,0:T(8,128)(2,1)}, u32[]{:S(2)}) copy-start(bf16[96,768]{1,0:T(8,128)(2,1)} %get-tuple-element.64) | copy-start | bytes 442372
  206.5 5.7 %copy-start.10 = (bf16[128,768]{0,1:T(8,128)(2,1)S(1)}, bf16[128,768]{0,1:T(8,128)(2,1)}, u32[]{:S(2)}) copy-start(bf16[128,768]{0,1:T(8,128)(2,1)} %copy-done.9) | copy-start | bytes 589828
  207.6 5.0 %copy-start.8 = (bf16[128,768]{0,1:T(8,128)(2,1)S(1)}, bf16[128,768]{0,1:T(8,128)(2,1)}, u32[]{:S(2)}) copy-start(bf16[128,768]{0,1:T(8,128)(2,1)} %copy-done.7) | copy-start | bytes 589828
  207.6 19.6 %all-to-all-start.3 = ((bf16[4,192,768]{2,1,0:T(8,128)(2,1)}), bf16[4,192,768]{2,1,0:T(8,128)(2,1)}, u32[]{:S(2)}, u32[]{:S(2)}) async-start(bf16[4,192,768]{2,1,0:T(8,128)(2,1)} %broadcast_in_dim.34), calls=%async_computation.4 | async-start | bytes 2359296 | tf_op jit(solution)/shard_map/all_to_all | solution.py:81
  228.6 24.4 %all-to-all-start.4 = ((bf16[128,8,288]{0,2,1:T(8,128)(2,1)}), bf16[128,8,288]{0,2,1:T(8,128)(2,1)}, u32[]{:S(2)}, u32[]{:S(2)}) async-start(bf16[128,8,288]{0,2,1:T(8,128)(2,1)} %bitcast.107), calls=%async_computation.5 | async-start | bytes 1179648 | tf_op jit(solution)/shard_map/all_to_all | solution.py:81
  232.8 5.2 %copy-start.18 = (f32[768]{0:T(1024)S(1)}, f32[768]{0:T(1024)}, u32[]{:S(2)}) copy-start(f32[768]{0:T(1024)} %get-tuple-element.42) | copy-start | bytes 9220
  232.8 7.2 %copy-start.16 = (f32[12,64]{1,0:T(8,128)S(1)}, f32[12,64]{1,0:T(8,128)}, u32[]{:S(2)}) copy-start(f32[12,64]{1,0:T(8,128)} %get-tuple-element.62) | copy-start | bytes 9220
  253.0 6.2 %copy-start.20 = (f32[128]{0:T(128)S(1)}, f32[128]{0:T(128)}, u32[]{:S(2)}) copy-start(f32[128]{0:T(128)} %copy-done.19) | copy-start | bytes 1540
  253.0 24.1 %all-to-all-start.7 = ((bf16[128,8,96]{0,2,1:T(8,128)(2,1)}), bf16[128,8,96]{0,2,1:T(8,128)(2,1)}, u32[]{:S(2)}, u32[]{:S(2)}) async-start(bf16[128,8,96]{0,2,1:T(8,128)(2,1)} %bitcast.109), calls=%async_computation.9 | async-start | bytes 393216 | tf_op jit(solution)/shard_map/all_to_all | solution.py:81
  257.1 79.9 %reduce-scatter.5.cloned.1.call-start = ((), (), s32[]{:S(2)}) async-start(), calls=%async_computation.18 | async-start | bytes 1769472 | tf_op jit(solution)/shard_map/reduce_scatter | solution.py:196
  259.2 4.3 %copy-start.31 = (f32[128]{0:T(128)S(1)}, f32[128]{0:T(128)}, u32[]{:S(2)}) copy-start(f32[128]{0:T(128)} %copy-done.30) | copy-start | bytes 1540
  259.2 4.3 %copy-start.24 = (f32[128]{0:T(128)S(1)}, f32[128]{0:T(128)}, u32[]{:S(2)}) copy-start(f32[128]{0:T(128)} %copy-done.23) | copy-start | bytes 1540
  259.2 4.6 %copy-start.4 = (f32[128,768]{1,0:T(8,128)S(1)}, f32[128,768]{1,0:T(8,128)}, u32[]{:S(2)}) copy-start(f32[128,768]{1,0:T(8,128)} %copy-done.3) | copy-start | bytes 1179652
  259.2 4.6 %copy-start.13 = (bf16[128,768]{1,0:T(8,128)(2,1)S(1)}, bf16[128,768]{1,0:T(8,128)(2,1)}, u32[]{:S(2)}) copy-start(bf16[128,768]{1,0:T(8,128)(2,1)} %param.29) | copy-start | bytes 589828
  259.2 4.6 %copy-start.21 = (f32[128]{0:T(128)S(1)}, f32[128]{0:T(128)}, u32[]{:S(2)}) copy-start(f32[128]{0:T(128)} %copy-done.19) | copy-start | bytes 1540
  259.2 4.6 %copy-start.28 = (f32[128]{0:T(128)S(1)}, f32[128]{0:T(128)}, u32[]{:S(2)}) copy-start(f32[128]{0:T(128)} %copy-done.27) | copy-start | bytes 1540
  277.1 10.9 %all-to-all-start.5 = ((f32[8,1,768]{2,1,0:T(1,128)}), f32[8,1,768]{2,1,0:T(1,128)S(1)}, u32[]{:S(2)}, u32[]{:S(2)}) async-start(f32[8,1,768]{2,1,0:T(1,128)} %all_to_all.113), calls=%async_computation.7 | async-start | bytes 49152 | tf_op jit(solution)/shard_map/all_to_all | solution.py:81
  282.1 2.0 copy-start.11
  284.1 8.1 %copy-start.26 = (f32[384]{0:T(512)S(1)}, f32[384]{0:T(512)}, u32[]{:S(2)}) copy-start(f32[384]{0:T(512)} %get-tuple-element.51) | copy-start | bytes 4612
  288.0 13.4 %all-to-all-start.8 = ((bf16[4,96,768]{2,1,0:T(8,128)(2,1)}), bf16[4,96,768]{2,1,0:T(8,128)(2,1)}, u32[]{:S(2)}, u32[]{:S(2)}) async-start(bf16[4,96,768]{2,1,0:T(8,128)(2,1)} %pad_maximum_fusion.2), calls=%async_computation.10 | async-start | bytes 1179648 | tf_op jit(solution)/shard_map/all_to_all | solution.py:81
  302.1 7.9 %all-to-all-start.6 = ((f32[4,1,1152]{2,1,0:T(1,128)}), f32[4,1,1152]{2,1,0:T(1,128)S(1)}, u32[]{:S(2)}, u32[]{:S(2)}) async-start(f32[4,1,1152]{2,1,0:T(1,128)} %broadcast_in_dim.37), calls=%async_computation.8 | async-start | bytes 36864 | tf_op jit(solution)/shard_map/all_to_all | solution.py:81
  310.0 11.0 %all-to-all-start.9 = ((bf16[8,24,288]{2,1,0:T(8,128)(2,1)}), bf16[8,24,288]{2,1,0:T(8,128)(2,1)}, u32[]{:S(2)}, u32[]{:S(2)}) async-start(bf16[8,24,288]{2,1,0:T(8,128)(2,1)} %all_to_all.109), calls=%async_computation.11 | async-start | bytes 294912 | tf_op jit(solution)/shard_map/all_to_all | solution.py:81
  323.1 12.0 %all-to-all-start.10 = ((bf16[4,96,768]{2,1,0:T(8,128)(2,1)}), bf16[4,96,768]{2,1,0:T(8,128)(2,1)S(1)}, u32[]{:S(2)}, u32[]{:S(2)}) async-start(bf16[4,96,768]{2,1,0:T(8,128)(2,1)} %broadcast_in_dim.68), calls=%async_computation.12 | async-start | bytes 1179648 | tf_op jit(solution)/shard_map/all_to_all | solution.py:81
  335.2 1.9 copy-start.17
  (4 other events, 2.8 us)
Sparse Core Ops, SparseCore 0:
  9.7 44.2 all-gather.7
  55.6 21.5 all-gather.9
  80.6 24.8 all-gather.11
  107.0 33.7 all-gather.13
  153.2 33.8 reduce-scatter.2
  188.6 26.5 all-gather.17
  217.4 27.5 all-gather.15
  260.3 35.7 reduce-scatter.4
